TPU v7x, 128 devices: a whole 4x4x4 slice. The times are simulated.
128 devices in a mesh: heads: 2 (over core), seq: 64 (over x, z, y).
Axes of the slice: x: 4, y: 4, z: 4, core: 2. Of those that a mesh axis runs over, the one named last changes fastest.
Arguments:
- tokens: bfloat16 [24576, 3072], P('seq', 'heads'), may hold values from -6 to 6
- w_query: bfloat16 [3072, 1536], P(None, 'heads'), may hold values from -1 to 1
- w_key: bfloat16 [3072, 1536], P(None, 'heads'), may hold values from -1 to 1
- w_value: bfloat16 [3072, 1536], P(None, 'heads'), may hold values from -0.109375 to 0.109375
- query_gain: float32 [128], replicated, may hold values from 0.5 to 8
- key_gain: float32 [128], replicated, may hold values from 0.5 to 8
- w_out: bfloat16 [1536, 3072], P('heads'), may hold values from -1.5 to 1.5
- key_tiles: int32 [64, 27], P('seq'), may hold values from 0 to 63, as said below
- key_counts: int32 [64], P('seq'), may hold values from 2 to 27, as said below
Outputs:
- mixed: bfloat16 [24576, 3072], P('seq', 'heads')
Inputs may be any that keep to these rules, and one draw needn't show every extreme that they name: `key_tiles`: every used id is a tile whose grid place differs from tile g's by at most one in each of the three grid coordinates; slot 0 is g itself; used ids of one list are distinct; unused slots hold g. `key_counts`: some tile in every draw uses all 27 slots, and some tile uses exactly 2.
All inputs are finite; a program needn't handle non-finite values.
Results may differ from a plain program's by a relative error of at most 0.0095.
The roundings to bfloat16 on the way count: a program that leaves them out, or rounds other values in their place, can miss the bound.
Values may be sent and summed in bfloat16 or wider, within the bound.
A program may use at most 256 MiB of HBM per device.

v0:
```python
import jax
import jax.numpy as jnp
from jax import lax
from jax.sharding import PartitionSpec as P

GRID_H = 4
GRID_W = 4


def passed_along(x, axis, by):
    count = lax.axis_size(axis)
    pairs = [(i, i + by) for i in range(count) if 0 <= i + by < count]
    return lax.ppermute(x, axis, pairs)


def normalize(proj, gain, heads):
    rows = proj.reshape(proj.shape[0], heads, -1)
    meansq = jnp.mean(rows * rows, axis=-1, keepdims=True)
    return (rows * lax.rsqrt(meansq + 1e-06) * gain).astype(jnp.bfloat16).reshape(proj.shape[0], -1)


def on_device(tokens, w_query, w_key, w_value, query_gain, key_gain, w_out, key_tiles, key_counts):
    head_size = query_gain.shape[0]
    width = w_query.shape[1]
    group = width // head_size
    tile_rows = tokens.shape[0]
    slots = key_tiles.shape[1]
    plane = GRID_H * GRID_W
    scale = 1.0 / head_size**0.5
    whole = lax.all_gather(tokens, "heads", axis=1, tiled=True)
    queries = normalize(
        jnp.dot(whole, w_query, preferred_element_type=jnp.float32), query_gain, group
    )
    keys = normalize(jnp.dot(whole, w_key, preferred_element_type=jnp.float32), key_gain, group)
    values = jnp.dot(whole, w_value, preferred_element_type=jnp.float32).astype(jnp.bfloat16)
    key_list = []
    value_list = []
    for code in range(27):
        step_f = code // 9 - 1
        step_h = code // 3 % 3 - 1
        step_w = code % 3 - 1
        offset = step_f * plane + step_h * GRID_W + step_w
        if code == 13:
            key_list.append(keys)
            value_list.append(values)
        else:
            moved_k, moved_v = passed_along((keys, values), "seq", -offset)
            key_list.append(moved_k)
            value_list.append(moved_v)
    stack_k = jnp.stack(key_list, axis=0)
    stack_v = jnp.stack(value_list, axis=0)
    mine = lax.axis_index("seq")
    ids = key_tiles[0]
    count = key_counts[0]
    codes = (
        (ids // plane - mine // plane + 1) * 9
        + (ids // GRID_W % GRID_H - mine // GRID_W % GRID_H + 1) * 3
        + (ids % GRID_W - mine % GRID_W + 1)
    )
    chosen_k = jnp.take(stack_k, codes, axis=0).reshape(slots * tile_rows, width)
    chosen_v = jnp.take(stack_v, codes, axis=0).reshape(slots * tile_rows, width)
    valid = jnp.arange(slots * tile_rows, dtype=jnp.int32) // tile_rows < count
    outputs = []
    for head in range(group):
        cols = slice(head * head_size, (head + 1) * head_size)
        score = (
            lax.dot_general(
                queries[:, cols],
                chosen_k[:, cols],
                (((1,), (1,)), ((), ())),
                preferred_element_type=jnp.float32,
            )
            * scale
        )
        score = jnp.where(valid[None, :], score, -jnp.inf)
        top = jnp.max(score, axis=-1, keepdims=True)
        expo = jnp.exp(score - top)
        total = jnp.sum(expo, axis=-1)
        summed = jnp.dot(
            expo.astype(jnp.bfloat16), chosen_v[:, cols], preferred_element_type=jnp.float32
        )
        outputs.append(summed / total[:, None])
    attended = jnp.concatenate(outputs, axis=1).astype(jnp.bfloat16)
    partial_out = jnp.dot(attended, w_out, preferred_element_type=jnp.float32)
    return lax.psum_scatter(
        partial_out.astype(jnp.bfloat16), "heads", scatter_dimension=1, tiled=True
    )


def solution(mesh):
    return jax.shard_map(
        on_device,
        mesh=mesh,
        in_specs=(
            P("seq", "heads"),
            P(None, "heads"),
            P(None, "heads"),
            P(None, "heads"),
            P(),
            P(),
            P("heads", None),
            P("seq", None),
            P("seq"),
        ),
        out_specs=P("seq", "heads"),
        check_vma=False,
    )
```

profile of v0, /device:TPU:1, one launch (start us, length us, event | category | flops | bytes accessed | tf_op | source)
XLA Modules:
  0.0 963.9 jit_solution(15942071822936124528)
XLA Ops:
  10.4 15.9 %all-gather.2.cloned.1.call-done = bf16[384,3072]{1,0:T(8,128)(2,1)} async-done(((bf16[384,1536]{1,0:T(8,128)(2,1)}), bf16[384,3072]{1,0:T(8,128)(2,1)}) %all-gather.2.cloned.1.call-update) | async-done | bytes 2359312 | tf_op jit(solution)/shard_map/all_gather | solution.py:30
  26.3 6.1 fusion.156
  34.9 6.0 collective-permute-start
  86.1 7.6 collective-permute-done.3
  99.0 7.4 collective-permute-done.4
  110.8 11.2 %collective-permute-start.10 = (bf16[384,768]{1,0:T(8,128)(2,1)S(1)}, bf16[384,768]{1,0:T(8,128)(2,1)S(1)}, u32[]{:S(2)}, u32[]{:S(2)}) collective-permute-start(bf16[384,768]{1,0:T(8,128)(2,1)S(1)} %multiply_convert_fusion), channel_id=1, source_target_pairs={{0,4},{1,5},{2,6},{3,7},{4,8},{5,9},{6,10},{7,11},{8,12},{9,13},{1... | collective-permute-start | bytes 1769480 | tf_op jit(solution)/shard_map/ppermute | solution.py:13
  122.9 10.5 %collective-permute-start.11 = (bf16[384,768]{1,0:T(8,128)(2,1)S(1)}, bf16[384,768]{1,0:T(8,128)(2,1)S(1)}, u32[]{:S(2)}, u32[]{:S(2)}) collective-permute-start(bf16[384,768]{1,0:T(8,128)(2,1)S(1)} %multiply_convert_fusion), channel_id=1, source_target_pairs={{0,3},{1,4},{2,5},{3,6},{4,7},{5,8},{6,9},{7,10},{8,11},{9,12},{10... | collective-permute-start | bytes 1769480 | tf_op jit(solution)/shard_map/ppermute | solution.py:13
  143.8 38.4 %collective-permute-start.26 = (bf16[384,768]{1,0:T(8,128)(2,1)S(1)}, bf16[384,768]{1,0:T(8,128)(2,1)S(1)}, u32[]{:S(2)}, u32[]{:S(2)}) collective-permute-start(bf16[384,768]{1,0:T(8,128)(2,1)S(1)} %convolution_convert_fusion.1), channel_id=1, source_target_pairs={{0,21},{1,22},{2,23},{3,24},{4,25},{5,26},{6,27},{7,28},{8,29},{9,... | collective-permute-start | bytes 1769480 | tf_op jit(solution)/shard_map/ppermute | solution.py:13
  183.2 15.9 %collective-permute-start.27 = (bf16[384,768]{1,0:T(8,128)(2,1)S(1)}, bf16[384,768]{1,0:T(8,128)(2,1)S(1)}, u32[]{:S(2)}, u32[]{:S(2)}) collective-permute-start(bf16[384,768]{1,0:T(8,128)(2,1)S(1)} %convolution_convert_fusion.1), channel_id=1, source_target_pairs={{0,20},{1,21},{2,22},{3,23},{4,24},{5,25},{6,26},{7,27},{8,28},{9,... | collective-permute-start | bytes 1769480 | tf_op jit(solution)/shard_map/ppermute | solution.py:13
  204.5 6.9 collective-permute-start.29
  212.7 15.2 %collective-permute-start.30 = (bf16[384,768]{1,0:T(8,128)(2,1)S(1)}, bf16[384,768]{1,0:T(8,128)(2,1)S(1)}, u32[]{:S(2)}, u32[]{:S(2)}) collective-permute-start(bf16[384,768]{1,0:T(8,128)(2,1)S(1)} %convolution_convert_fusion.1), channel_id=1, source_target_pairs={{0,16},{1,17},{2,18},{3,19},{4,20},{5,21},{6,22},{7,23},{8,24},{9,... | collective-permute-start | bytes 1769480 | tf_op jit(solution)/shard_map/ppermute | solution.py:13
  228.8 26.9 %collective-permute-start.31 = (bf16[384,768]{1,0:T(8,128)(2,1)S(1)}, bf16[384,768]{1,0:T(8,128)(2,1)S(1)}, u32[]{:S(2)}, u32[]{:S(2)}) collective-permute-start(bf16[384,768]{1,0:T(8,128)(2,1)S(1)} %convolution_convert_fusion.1), channel_id=1, source_target_pairs={{0,15},{1,16},{2,17},{3,18},{4,19},{5,20},{6,21},{7,22},{8,23},{9,... | collective-permute-start | bytes 1769480 | tf_op jit(solution)/shard_map/ppermute | solution.py:13
  256.6 10.6 %collective-permute-start.32 = (bf16[384,768]{1,0:T(8,128)(2,1)S(1)}, bf16[384,768]{1,0:T(8,128)(2,1)S(1)}, u32[]{:S(2)}, u32[]{:S(2)}) collective-permute-start(bf16[384,768]{1,0:T(8,128)(2,1)S(1)} %convolution_convert_fusion.1), channel_id=1, source_target_pairs={{0,13},{1,14},{2,15},{3,16},{4,17},{5,18},{6,19},{7,20},{8,21},{9,... | collective-permute-start | bytes 1769480 | tf_op jit(solution)/shard_map/ppermute | solution.py:13
  268.0 14.0 %collective-permute-start.33 = (bf16[384,768]{1,0:T(8,128)(2,1)S(1)}, bf16[384,768]{1,0:T(8,128)(2,1)S(1)}, u32[]{:S(2)}, u32[]{:S(2)}) collective-permute-start(bf16[384,768]{1,0:T(8,128)(2,1)S(1)} %convolution_convert_fusion.1), channel_id=1, source_target_pairs={{0,12},{1,13},{2,14},{3,15},{4,16},{5,17},{6,18},{7,19},{8,20},{9,... | collective-permute-start | bytes 1769480 | tf_op jit(solution)/shard_map/ppermute | solution.py:13
  283.0 9.9 %collective-permute-start.34 = (bf16[384,768]{1,0:T(8,128)(2,1)S(1)}, bf16[384,768]{1,0:T(8,128)(2,1)S(1)}, u32[]{:S(2)}, u32[]{:S(2)}) collective-permute-start(bf16[384,768]{1,0:T(8,128)(2,1)S(1)} %convolution_convert_fusion.1), channel_id=1, source_target_pairs={{0,11},{1,12},{2,13},{3,14},{4,15},{5,16},{6,17},{7,18},{8,19},{9,... | collective-permute-start | bytes 1769480 | tf_op jit(solution)/shard_map/ppermute | solution.py:13
  304.9 20.0 %collective-permute-start.37 = (bf16[384,768]{1,0:T(8,128)(2,1)S(1)}, bf16[384,768]{1,0:T(8,128)(2,1)S(1)}, u32[]{:S(2)}, u32[]{:S(2)}) collective-permute-start(bf16[384,768]{1,0:T(8,128)(2,1)S(1)} %convolution_convert_fusion.1), channel_id=1, source_target_pairs={{0,3},{1,4},{2,5},{3,6},{4,7},{5,8},{6,9},{7,10},{8,11},{9,12},{10... | collective-permute-start | bytes 1769480 | tf_op jit(solution)/shard_map/ppermute | solution.py:13
  353.2 13.8 %collective-permute-done.16 = bf16[384,768]{1,0:T(8,128)(2,1)S(1)} collective-permute-done((bf16[384,768]{1,0:T(8,128)(2,1)S(1)}, bf16[384,768]{1,0:T(8,128)(2,1)S(1)}, u32[]{:S(2)}, u32[]{:S(2)}) %collective-permute-start.16) | collective-permute-done | bytes 589856 | tf_op jit(solution)/shard_map/ppermute | solution.py:13
  369.1 20.8 %collective-permute-done.17 = bf16[384,768]{1,0:T(8,128)(2,1)S(1)} collective-permute-done((bf16[384,768]{1,0:T(8,128)(2,1)S(1)}, bf16[384,768]{1,0:T(8,128)(2,1)S(1)}, u32[]{:S(2)}, u32[]{:S(2)}) %collective-permute-start.17) | collective-permute-done | bytes 589856 | tf_op jit(solution)/shard_map/ppermute | solution.py:13
  392.1 18.7 %collective-permute-done.18 = bf16[384,768]{1,0:T(8,128)(2,1)S(1)} collective-permute-done((bf16[384,768]{1,0:T(8,128)(2,1)S(1)}, bf16[384,768]{1,0:T(8,128)(2,1)S(1)}, u32[]{:S(2)}, u32[]{:S(2)}) %collective-permute-start.18) | collective-permute-done | bytes 589856 | tf_op jit(solution)/shard_map/ppermute | solution.py:13
  412.9 28.4 %collective-permute-done.19 = bf16[384,768]{1,0:T(8,128)(2,1)S(1)} collective-permute-done((bf16[384,768]{1,0:T(8,128)(2,1)S(1)}, bf16[384,768]{1,0:T(8,128)(2,1)S(1)}, u32[]{:S(2)}, u32[]{:S(2)}) %collective-permute-start.19) | collective-permute-done | bytes 589856 | tf_op jit(solution)/shard_map/ppermute | solution.py:13
  445.6 79.9 %collective-permute-done.21 = bf16[384,768]{1,0:T(8,128)(2,1)S(1)} collective-permute-done((bf16[384,768]{1,0:T(8,128)(2,1)S(1)}, bf16[384,768]{1,0:T(8,128)(2,1)S(1)}, u32[]{:S(2)}, u32[]{:S(2)}) %collective-permute-start.21) | collective-permute-done | bytes 589856 | tf_op jit(solution)/shard_map/ppermute | solution.py:13
  534.1 33.9 %collective-permute-done.25 = bf16[384,768]{1,0:T(8,128)(2,1)S(1)} collective-permute-done((bf16[384,768]{1,0:T(8,128)(2,1)S(1)}, bf16[384,768]{1,0:T(8,128)(2,1)S(1)}, u32[]{:S(2)}, u32[]{:S(2)}) %collective-permute-start.25) | collective-permute-done | bytes 589856 | tf_op jit(solution)/shard_map/ppermute | solution.py:13
  589.5 37.2 %collective-permute-done.44 = bf16[384,768]{1,0:T(8,128)(2,1)S(1)} collective-permute-done((bf16[384,768]{1,0:T(8,128)(2,1)S(1)}, bf16[384,768]{1,0:T(8,128)(2,1)S(1)}, u32[]{:S(2)}, u32[]{:S(2)}) %collective-permute-start.44) | collective-permute-done | bytes 589856 | tf_op jit(solution)/shard_map/ppermute | solution.py:13
  633.2 71.8 %collective-permute-done.47 = bf16[384,768]{1,0:T(8,128)(2,1)S(1)} collective-permute-done((bf16[384,768]{1,0:T(8,128)(2,1)S(1)}, bf16[384,768]{1,0:T(8,128)(2,1)S(1)}, u32[]{:S(2)}, u32[]{:S(2)}) %collective-permute-start.47) | collective-permute-done | bytes 589856 | tf_op jit(solution)/shard_map/ppermute | solution.py:13
  706.8 12.6 %gather_fusion = bf16[27,384,768]{2,1,0:T(8,128)(2,1)} fusion(bf16[27,384,768]{2,1,0:T(8,128)(2,1)} %bitcast_dynamic-update-slice_fusion.27, s32[1024]{0:T(1024)} %pad_clamp_fusion), kind=kCustom, calls=%fused_computation.clone | custom fusion | bytes 31850604 | tf_op jit(solution)/shard_map/jit(_take)/gather | solution.py:60
  719.4 8.1 collective-permute-done.49
  728.3 17.5 %collective-permute-done.50 = bf16[384,768]{1,0:T(8,128)(2,1)S(1)} collective-permute-done((bf16[384,768]{1,0:T(8,128)(2,1)S(1)}, bf16[384,768]{1,0:T(8,128)(2,1)S(1)}, u32[]{:S(2)}, u32[]{:S(2)}) %collective-permute-start.50) | collective-permute-done | bytes 589856 | tf_op jit(solution)/shard_map/ppermute | solution.py:13
  747.5 12.7 %gather_fusion.1 = bf16[27,384,768]{2,1,0:T(8,128)(2,1)} fusion(bf16[27,384,768]{2,1,0:T(8,128)(2,1)} %bitcast_dynamic-update-slice_fusion, s32[1024]{0:T(1024)} %pad_clamp_fusion), kind=kCustom, calls=%fused_computation.1.clone | custom fusion | bytes 31850604 | tf_op jit(solution)/shard_map/jit(_take)/gather | solution.py:61
  760.2 17.4 %broadcast_select_fusion.1 = (bf16[27,384,768]{2,1,0:T(8,128)(2,1)S(1)}, bf16[27,384,768]{2,1,0:T(8,128)(2,1)}) fusion(bf16[27,384,768]{2,1,0:T(8,128)(2,1)} %gather_fusion, pred[27]{0:T(512)(128)(4,1)S(1)} %copy-done.2, bf16[27,384,768]{2,1,0:T(8,128)(2,1)} %gather_fusion.1), kind=kLoop, calls=%fused_computation.21 | loop fusion | flops 15925248 | bytes 63701020 | tf_op jit(solution)/shard_map/jit(_take)/select_n | solution.py:60
  777.6 6.8 fusion.158
  784.4 7.0 fusion.159
  791.4 6.9 fusion.160
  798.3 6.9 fusion.161
  805.2 6.9 fusion.162
  812.1 15.5 %fusion.163 = (f32[384]{0:T(512)S(1)}, f32[384,10368]{1,0:T(8,128)}) fusion(bf16[10368,768]{1,0:T(8,128)(2,1)S(1)} %bitcast.158, bf16[384,768]{1,0:T(8,128)(2,1)S(1)} %multiply_convert_fusion.1, pred[10368]{0:T(1024)(128)(4,1)S(1)} %fusion.144), kind=kOutput, calls=%fused_computation.183 | convolution fusion | flops 1031159424 | bytes 18690560 | tf_op jit(solution)/shard_map/dot_general | solution.py:67
  827.6 7.8 fusion.6
  835.4 8.6 fusion.58
  844.0 7.8 fusion.8
  851.7 8.6 fusion.73
  860.3 7.8 fusion.10
  868.1 8.8 fusion.88
  876.9 7.8 fusion.12
  884.7 8.6 fusion.103
  893.3 7.8 fusion.14
  901.0 8.6 fusion.118
  909.7 8.2 fusion.16
  917.8 8.7 fusion.133
  930.0 26.6 %reduce-scatter.2.cloned.1.call-done = bf16[384,1536]{1,0:T(8,128)(2,1)} async-done(((bf16[384,3072]{1,0:T(8,128)(2,1)}), bf16[384,1536]{1,0:T(8,128)(2,1)}) %reduce-scatter.2.cloned.1.call-update) | async-done | bytes 1179664 | tf_op jit(solution)/shard_map/reduce_scatter | solution.py:85
  (171 shorter events, 178.2 us)
Async XLA Ops:
  7.3 949.4 %reduce-scatter.2.cloned.1.call-start = ((), (), s32[]{:S(2)}) async-start(), calls=%async_computation.2 | async-start | bytes 3538944 | tf_op jit(solution)/shard_map/reduce_scatter | solution.py:85
  34.9 32.6 %collective-permute-start = (bf16[384,768]{1,0:T(8,128)(2,1)S(1)}, bf16[384,768]{1,0:T(8,128)(2,1)}, u32[]{:S(2)}, u32[]{:S(2)}) collective-permute-start(bf16[384,768]{1,0:T(8,128)(2,1)S(1)} %multiply_convert_fusion), channel_id=1, source_target_pairs={{0,21},{1,22},{2,23},{3,24},{4,25},{5,26},{6,27},{7,28},{8,29},{9,... | collective-permute-start | bytes 1769480 | tf_op jit(solution)/shard_map/ppermute | solution.py:13
  40.9 32.5 %collective-permute-start.1 = (bf16[384,768]{1,0:T(8,128)(2,1)S(1)}, bf16[384,768]{1,0:T(8,128)(2,1)}, u32[]{:S(2)}, u32[]{:S(2)}) collective-permute-start(bf16[384,768]{1,0:T(8,128)(2,1)S(1)} %multiply_convert_fusion), channel_id=1, source_target_pairs={{0,20},{1,21},{2,22},{3,23},{4,24},{5,25},{6,26},{7,27},{8,28},{9,... | collective-permute-start | bytes 1769480 | tf_op jit(solution)/shard_map/ppermute | solution.py:13
  45.8 35.2 %collective-permute-start.2 = (bf16[384,768]{1,0:T(8,128)(2,1)S(1)}, bf16[384,768]{1,0:T(8,128)(2,1)}, u32[]{:S(2)}, u32[]{:S(2)}) collective-permute-start(bf16[384,768]{1,0:T(8,128)(2,1)S(1)} %multiply_convert_fusion), channel_id=1, source_target_pairs={{0,19},{1,20},{2,21},{3,22},{4,23},{5,24},{6,25},{7,26},{8,27},{9,... | collective-permute-start | bytes 1769480 | tf_op jit(solution)/shard_map/ppermute | solution.py:13
  50.5 43.2 %collective-permute-start.3 = (bf16[384,768]{1,0:T(8,128)(2,1)S(1)}, bf16[384,768]{1,0:T(8,128)(2,1)}, u32[]{:S(2)}, u32[]{:S(2)}) collective-permute-start(bf16[384,768]{1,0:T(8,128)(2,1)S(1)} %multiply_convert_fusion), channel_id=1, source_target_pairs={{0,17},{1,18},{2,19},{3,20},{4,21},{5,22},{6,23},{7,24},{8,25},{9,... | collective-permute-start | bytes 1769480 | tf_op jit(solution)/shard_map/ppermute | solution.py:13
  52.6 53.8 %collective-permute-start.4 = (bf16[384,768]{1,0:T(8,128)(2,1)S(1)}, bf16[384,768]{1,0:T(8,128)(2,1)}, u32[]{:S(2)}, u32[]{:S(2)}) collective-permute-start(bf16[384,768]{1,0:T(8,128)(2,1)S(1)} %multiply_convert_fusion), channel_id=1, source_target_pairs={{0,16},{1,17},{2,18},{3,19},{4,20},{5,21},{6,22},{7,23},{8,24},{9,... | collective-permute-start | bytes 1769480 | tf_op jit(solution)/shard_map/ppermute | solution.py:13
  67.5 43.3 %collective-permute-start.5 = (bf16[384,768]{1,0:T(8,128)(2,1)S(1)}, bf16[384,768]{1,0:T(8,128)(2,1)S(1)}, u32[]{:S(2)}, u32[]{:S(2)}) collective-permute-start(bf16[384,768]{1,0:T(8,128)(2,1)S(1)} %multiply_convert_fusion), channel_id=1, source_target_pairs={{0,15},{1,16},{2,17},{3,18},{4,19},{5,20},{6,21},{7,22},{8,23},{9,... | collective-permute-start | bytes 1769480 | tf_op jit(solution)/shard_map/ppermute | solution.py:13
  73.4 49.5 %collective-permute-start.6 = (bf16[384,768]{1,0:T(8,128)(2,1)S(1)}, bf16[384,768]{1,0:T(8,128)(2,1)S(1)}, u32[]{:S(2)}, u32[]{:S(2)}) collective-permute-start(bf16[384,768]{1,0:T(8,128)(2,1)S(1)} %multiply_convert_fusion), channel_id=1, source_target_pairs={{0,13},{1,14},{2,15},{3,16},{4,17},{5,18},{6,19},{7,20},{8,21},{9,... | collective-permute-start | bytes 1769480 | tf_op jit(solution)/shard_map/ppermute | solution.py:13
  81.0 53.3 %collective-permute-start.7 = (bf16[384,768]{1,0:T(8,128)(2,1)S(1)}, bf16[384,768]{1,0:T(8,128)(2,1)S(1)}, u32[]{:S(2)}, u32[]{:S(2)}) collective-permute-start(bf16[384,768]{1,0:T(8,128)(2,1)S(1)} %multiply_convert_fusion), channel_id=1, source_target_pairs={{0,12},{1,13},{2,14},{3,15},{4,16},{5,17},{6,18},{7,19},{8,20},{9,... | collective-permute-start | bytes 1769480 | tf_op jit(solution)/shard_map/ppermute | solution.py:13
  93.7 45.8 %collective-permute-start.8 = (bf16[384,768]{1,0:T(8,128)(2,1)S(1)}, bf16[384,768]{1,0:T(8,128)(2,1)S(1)}, u32[]{:S(2)}, u32[]{:S(2)}) collective-permute-start(bf16[384,768]{1,0:T(8,128)(2,1)S(1)} %multiply_convert_fusion), channel_id=1, source_target_pairs={{0,11},{1,12},{2,13},{3,14},{4,15},{5,16},{6,17},{7,18},{8,19},{9,... | collective-permute-start | bytes 1769480 | tf_op jit(solution)/shard_map/ppermute | solution.py:13
  106.4 35.3 %collective-permute-start.9 = (bf16[384,768]{1,0:T(8,128)(2,1)S(1)}, bf16[384,768]{1,0:T(8,128)(2,1)S(1)}, u32[]{:S(2)}, u32[]{:S(2)}) collective-permute-start(bf16[384,768]{1,0:T(8,128)(2,1)S(1)} %multiply_convert_fusion), channel_id=1, source_target_pairs={{0,5},{1,6},{2,7},{3,8},{4,9},{5,10},{6,11},{7,12},{8,13},{9,14},{... | collective-permute-start | bytes 1769480 | tf_op jit(solution)/shard_map/ppermute | solution.py:13
  110.8 33.0 %collective-permute-start.10 = (bf16[384,768]{1,0:T(8,128)(2,1)S(1)}, bf16[384,768]{1,0:T(8,128)(2,1)S(1)}, u32[]{:S(2)}, u32[]{:S(2)}) collective-permute-start(bf16[384,768]{1,0:T(8,128)(2,1)S(1)} %multiply_convert_fusion), channel_id=1, source_target_pairs={{0,4},{1,5},{2,6},{3,7},{4,8},{5,9},{6,10},{7,11},{8,12},{9,13},{1... | collective-permute-start | bytes 1769480 | tf_op jit(solution)/shard_map/ppermute | solution.py:13
  122.9 60.2 %collective-permute-start.11 = (bf16[384,768]{1,0:T(8,128)(2,1)S(1)}, bf16[384,768]{1,0:T(8,128)(2,1)S(1)}, u32[]{:S(2)}, u32[]{:S(2)}) collective-permute-start(bf16[384,768]{1,0:T(8,128)(2,1)S(1)} %multiply_convert_fusion), channel_id=1, source_target_pairs={{0,3},{1,4},{2,5},{3,6},{4,7},{5,8},{6,9},{7,10},{8,11},{9,12},{10... | collective-permute-start | bytes 1769480 | tf_op jit(solution)/shard_map/ppermute | solution.py:13
  134.3 65.6 %collective-permute-start.12 = (bf16[384,768]{1,0:T(8,128)(2,1)S(1)}, bf16[384,768]{1,0:T(8,128)(2,1)S(1)}, u32[]{:S(2)}, u32[]{:S(2)}) collective-permute-start(bf16[384,768]{1,0:T(8,128)(2,1)S(1)} %multiply_convert_fusion), channel_id=1, source_target_pairs={{0,1},{1,2},{2,3},{3,4},{4,5},{5,6},{6,7},{7,8},{8,9},{9,10},{10,1... | collective-permute-start | bytes 1769480 | tf_op jit(solution)/shard_map/ppermute | solution.py:13
  139.5 201.7 %collective-permute-start.13 = (bf16[384,768]{1,0:T(8,128)(2,1)S(1)}, bf16[384,768]{1,0:T(8,128)(2,1)S(1)}, u32[]{:S(2)}, u32[]{:S(2)}) collective-permute-start(bf16[384,768]{1,0:T(8,128)(2,1)S(1)} %multiply_convert_fusion), channel_id=1, source_target_pairs={{1,0},{2,1},{3,2},{4,3},{5,4},{6,5},{7,6},{8,7},{9,8},{10,9},{11,1... | collective-permute-start | bytes 1769480 | tf_op jit(solution)/shard_map/ppermute | solution.py:13
  141.7 201.7 %collective-permute-start.14 = (bf16[384,768]{1,0:T(8,128)(2,1)S(1)}, bf16[384,768]{1,0:T(8,128)(2,1)S(1)}, u32[]{:S(2)}, u32[]{:S(2)}) collective-permute-start(bf16[384,768]{1,0:T(8,128)(2,1)S(1)} %multiply_convert_fusion), channel_id=1, source_target_pairs={{3,0},{4,1},{5,2},{6,3},{7,4},{8,5},{9,6},{10,7},{11,8},{12,9},{13... | collective-permute-start | bytes 1769480 | tf_op jit(solution)/shard_map/ppermute | solution.py:13
  143.8 60.6 %collective-permute-start.26 = (bf16[384,768]{1,0:T(8,128)(2,1)S(1)}, bf16[384,768]{1,0:T(8,128)(2,1)S(1)}, u32[]{:S(2)}, u32[]{:S(2)}) collective-permute-start(bf16[384,768]{1,0:T(8,128)(2,1)S(1)} %convolution_convert_fusion.1), channel_id=1, source_target_pairs={{0,21},{1,22},{2,23},{3,24},{4,25},{5,26},{6,27},{7,28},{8,29},{9,... | collective-permute-start | bytes 1769480 | tf_op jit(solution)/shard_map/ppermute | solution.py:13
  183.2 29.5 %collective-permute-start.27 = (bf16[384,768]{1,0:T(8,128)(2,1)S(1)}, bf16[384,768]{1,0:T(8,128)(2,1)S(1)}, u32[]{:S(2)}, u32[]{:S(2)}) collective-permute-start(bf16[384,768]{1,0:T(8,128)(2,1)S(1)} %convolution_convert_fusion.1), channel_id=1, source_target_pairs={{0,20},{1,21},{2,22},{3,23},{4,24},{5,25},{6,26},{7,27},{8,28},{9,... | collective-permute-start | bytes 1769480 | tf_op jit(solution)/shard_map/ppermute | solution.py:13
  204.5 52.1 %collective-permute-start.29 = (bf16[384,768]{1,0:T(8,128)(2,1)S(1)}, bf16[384,768]{1,0:T(8,128)(2,1)S(1)}, u32[]{:S(2)}, u32[]{:S(2)}) collective-permute-start(bf16[384,768]{1,0:T(8,128)(2,1)S(1)} %convolution_convert_fusion.1), channel_id=1, source_target_pairs={{0,17},{1,18},{2,19},{3,20},{4,21},{5,22},{6,23},{7,24},{8,25},{9,... | collective-permute-start | bytes 1769480 | tf_op jit(solution)/shard_map/ppermute | solution.py:13
  212.7 55.4 %collective-permute-start.30 = (bf16[384,768]{1,0:T(8,128)(2,1)S(1)}, bf16[384,768]{1,0:T(8,128)(2,1)S(1)}, u32[]{:S(2)}, u32[]{:S(2)}) collective-permute-start(bf16[384,768]{1,0:T(8,128)(2,1)S(1)} %convolution_convert_fusion.1), channel_id=1, source_target_pairs={{0,16},{1,17},{2,18},{3,19},{4,20},{5,21},{6,22},{7,23},{8,24},{9,... | collective-permute-start | bytes 1769480 | tf_op jit(solution)/shard_map/ppermute | solution.py:13
  228.8 54.2 %collective-permute-start.31 = (bf16[384,768]{1,0:T(8,128)(2,1)S(1)}, bf16[384,768]{1,0:T(8,128)(2,1)S(1)}, u32[]{:S(2)}, u32[]{:S(2)}) collective-permute-start(bf16[384,768]{1,0:T(8,128)(2,1)S(1)} %convolution_convert_fusion.1), channel_id=1, source_target_pairs={{0,15},{1,16},{2,17},{3,18},{4,19},{5,20},{6,21},{7,22},{8,23},{9,... | collective-permute-start | bytes 1769480 | tf_op jit(solution)/shard_map/ppermute | solution.py:13
  256.6 37.1 %collective-permute-start.32 = (bf16[384,768]{1,0:T(8,128)(2,1)S(1)}, bf16[384,768]{1,0:T(8,128)(2,1)S(1)}, u32[]{:S(2)}, u32[]{:S(2)}) collective-permute-start(bf16[384,768]{1,0:T(8,128)(2,1)S(1)} %convolution_convert_fusion.1), channel_id=1, source_target_pairs={{0,13},{1,14},{2,15},{3,16},{4,17},{5,18},{6,19},{7,20},{8,21},{9,... | collective-permute-start | bytes 1769480 | tf_op jit(solution)/shard_map/ppermute | solution.py:13
  268.0 31.3 %collective-permute-start.33 = (bf16[384,768]{1,0:T(8,128)(2,1)S(1)}, bf16[384,768]{1,0:T(8,128)(2,1)S(1)}, u32[]{:S(2)}, u32[]{:S(2)}) collective-permute-start(bf16[384,768]{1,0:T(8,128)(2,1)S(1)} %convolution_convert_fusion.1), channel_id=1, source_target_pairs={{0,12},{1,13},{2,14},{3,15},{4,16},{5,17},{6,18},{7,19},{8,20},{9,... | collective-permute-start | bytes 1769480 | tf_op jit(solution)/shard_map/ppermute | solution.py:13
  293.7 32.1 %collective-permute-start.35 = (bf16[384,768]{1,0:T(8,128)(2,1)S(1)}, bf16[384,768]{1,0:T(8,128)(2,1)S(1)}, u32[]{:S(2)}, u32[]{:S(2)}) collective-permute-start(bf16[384,768]{1,0:T(8,128)(2,1)S(1)} %convolution_convert_fusion.1), channel_id=1, source_target_pairs={{0,5},{1,6},{2,7},{3,8},{4,9},{5,10},{6,11},{7,12},{8,13},{9,14},{... | collective-permute-start | bytes 1769480 | tf_op jit(solution)/shard_map/ppermute | solution.py:13
  299.3 34.3 %collective-permute-start.36 = (bf16[384,768]{1,0:T(8,128)(2,1)S(1)}, bf16[384,768]{1,0:T(8,128)(2,1)S(1)}, u32[]{:S(2)}, u32[]{:S(2)}) collective-permute-start(bf16[384,768]{1,0:T(8,128)(2,1)S(1)} %convolution_convert_fusion.1), channel_id=1, source_target_pairs={{0,4},{1,5},{2,6},{3,7},{4,8},{5,9},{6,10},{7,11},{8,12},{9,13},{1... | collective-permute-start | bytes 1769480 | tf_op jit(solution)/shard_map/ppermute | solution.py:13
  304.9 30.9 %collective-permute-start.37 = (bf16[384,768]{1,0:T(8,128)(2,1)S(1)}, bf16[384,768]{1,0:T(8,128)(2,1)S(1)}, u32[]{:S(2)}, u32[]{:S(2)}) collective-permute-start(bf16[384,768]{1,0:T(8,128)(2,1)S(1)} %convolution_convert_fusion.1), channel_id=1, source_target_pairs={{0,3},{1,4},{2,5},{3,6},{4,7},{5,8},{6,9},{7,10},{8,11},{9,12},{10... | collective-permute-start | bytes 1769480 | tf_op jit(solution)/shard_map/ppermute | solution.py:13
  335.8 31.2 %collective-permute-start.16 = (bf16[384,768]{1,0:T(8,128)(2,1)S(1)}, bf16[384,768]{1,0:T(8,128)(2,1)S(1)}, u32[]{:S(2)}, u32[]{:S(2)}) collective-permute-start(bf16[384,768]{1,0:T(8,128)(2,1)S(1)} %multiply_convert_fusion), channel_id=1, source_target_pairs={{5,0},{6,1},{7,2},{8,3},{9,4},{10,5},{11,6},{12,7},{13,8},{14,9},{... | collective-permute-start | bytes 1769480 | tf_op jit(solution)/shard_map/ppermute | solution.py:13
  338.2 51.7 %collective-permute-start.17 = (bf16[384,768]{1,0:T(8,128)(2,1)S(1)}, bf16[384,768]{1,0:T(8,128)(2,1)S(1)}, u32[]{:S(2)}, u32[]{:S(2)}) collective-permute-start(bf16[384,768]{1,0:T(8,128)(2,1)S(1)} %multiply_convert_fusion), channel_id=1, source_target_pairs={{11,0},{12,1},{13,2},{14,3},{15,4},{16,5},{17,6},{18,7},{19,8},{20... | collective-permute-start | bytes 1769480 | tf_op jit(solution)/shard_map/ppermute | solution.py:13
  341.2 69.6 %collective-permute-start.18 = (bf16[384,768]{1,0:T(8,128)(2,1)S(1)}, bf16[384,768]{1,0:T(8,128)(2,1)S(1)}, u32[]{:S(2)}, u32[]{:S(2)}) collective-permute-start(bf16[384,768]{1,0:T(8,128)(2,1)S(1)} %multiply_convert_fusion), channel_id=1, source_target_pairs={{12,0},{13,1},{14,2},{15,3},{16,4},{17,5},{18,6},{19,7},{20,8},{21... | collective-permute-start | bytes 1769480 | tf_op jit(solution)/shard_map/ppermute | solution.py:13
  343.4 97.9 %collective-permute-start.19 = (bf16[384,768]{1,0:T(8,128)(2,1)S(1)}, bf16[384,768]{1,0:T(8,128)(2,1)S(1)}, u32[]{:S(2)}, u32[]{:S(2)}) collective-permute-start(bf16[384,768]{1,0:T(8,128)(2,1)S(1)} %multiply_convert_fusion), channel_id=1, source_target_pairs={{13,0},{14,1},{15,2},{16,3},{17,4},{18,5},{19,6},{20,7},{21,8},{22... | collective-permute-start | bytes 1769480 | tf_op jit(solution)/shard_map/ppermute | solution.py:13
  351.0 92.4 %collective-permute-start.20 = (bf16[384,768]{1,0:T(8,128)(2,1)S(1)}, bf16[384,768]{1,0:T(8,128)(2,1)S(1)}, u32[]{:S(2)}, u32[]{:S(2)}) collective-permute-start(bf16[384,768]{1,0:T(8,128)(2,1)S(1)} %multiply_convert_fusion), channel_id=1, source_target_pairs={{15,0},{16,1},{17,2},{18,3},{19,4},{20,5},{21,6},{22,7},{23,8},{24... | collective-permute-start | bytes 1769480 | tf_op jit(solution)/shard_map/ppermute | solution.py:13
  367.0 158.5 %collective-permute-start.21 = (bf16[384,768]{1,0:T(8,128)(2,1)S(1)}, bf16[384,768]{1,0:T(8,128)(2,1)S(1)}, u32[]{:S(2)}, u32[]{:S(2)}) collective-permute-start(bf16[384,768]{1,0:T(8,128)(2,1)S(1)} %multiply_convert_fusion), channel_id=1, source_target_pairs={{16,0},{17,1},{18,2},{19,3},{20,4},{21,5},{22,6},{23,7},{24,8},{25... | collective-permute-start | bytes 1769480 | tf_op jit(solution)/shard_map/ppermute | solution.py:13
  389.9 137.8 %collective-permute-start.22 = (bf16[384,768]{1,0:T(8,128)(2,1)S(1)}, bf16[384,768]{1,0:T(8,128)(2,1)S(1)}, u32[]{:S(2)}, u32[]{:S(2)}) collective-permute-start(bf16[384,768]{1,0:T(8,128)(2,1)S(1)} %multiply_convert_fusion), channel_id=1, source_target_pairs={{17,0},{18,1},{19,2},{20,3},{21,4},{22,5},{23,6},{24,7},{25,8},{26... | collective-permute-start | bytes 1769480 | tf_op jit(solution)/shard_map/ppermute | solution.py:13
  410.8 119.1 %collective-permute-start.23 = (bf16[384,768]{1,0:T(8,128)(2,1)S(1)}, bf16[384,768]{1,0:T(8,128)(2,1)S(1)}, u32[]{:S(2)}, u32[]{:S(2)}) collective-permute-start(bf16[384,768]{1,0:T(8,128)(2,1)S(1)} %multiply_convert_fusion), channel_id=1, source_target_pairs={{19,0},{20,1},{21,2},{22,3},{23,4},{24,5},{25,6},{26,7},{27,8},{28... | collective-permute-start | bytes 1769480 | tf_op jit(solution)/shard_map/ppermute | solution.py:13
  441.3 90.7 %collective-permute-start.24 = (bf16[384,768]{1,0:T(8,128)(2,1)S(1)}, bf16[384,768]{1,0:T(8,128)(2,1)S(1)}, u32[]{:S(2)}, u32[]{:S(2)}) collective-permute-start(bf16[384,768]{1,0:T(8,128)(2,1)S(1)} %multiply_convert_fusion), channel_id=1, source_target_pairs={{20,0},{21,1},{22,2},{23,3},{24,4},{25,5},{26,6},{27,7},{28,8},{29... | collective-permute-start | bytes 1769480 | tf_op jit(solution)/shard_map/ppermute | solution.py:13
  443.4 124.6 %collective-permute-start.25 = (bf16[384,768]{1,0:T(8,128)(2,1)S(1)}, bf16[384,768]{1,0:T(8,128)(2,1)S(1)}, u32[]{:S(2)}, u32[]{:S(2)}) collective-permute-start(bf16[384,768]{1,0:T(8,128)(2,1)S(1)} %multiply_convert_fusion), channel_id=1, source_target_pairs={{21,0},{22,1},{23,2},{24,3},{25,4},{26,5},{27,6},{28,7},{29,8},{30... | collective-permute-start | bytes 1769480 | tf_op jit(solution)/shard_map/ppermute | solution.py:13
  525.5 44.7 %collective-permute-start.39 = (bf16[384,768]{1,0:T(8,128)(2,1)S(1)}, bf16[384,768]{1,0:T(8,128)(2,1)S(1)}, u32[]{:S(2)}, u32[]{:S(2)}) collective-permute-start(bf16[384,768]{1,0:T(8,128)(2,1)S(1)} %convolution_convert_fusion.1), channel_id=1, source_target_pairs={{1,0},{2,1},{3,2},{4,3},{5,4},{6,5},{7,6},{8,7},{9,8},{10,9},{11,1... | collective-permute-start | bytes 1769480 | tf_op jit(solution)/shard_map/ppermute | solution.py:13
  527.7 44.7 %collective-permute-start.40 = (bf16[384,768]{1,0:T(8,128)(2,1)S(1)}, bf16[384,768]{1,0:T(8,128)(2,1)S(1)}, u32[]{:S(2)}, u32[]{:S(2)}) collective-permute-start(bf16[384,768]{1,0:T(8,128)(2,1)S(1)} %convolution_convert_fusion.1), channel_id=1, source_target_pairs={{3,0},{4,1},{5,2},{6,3},{7,4},{8,5},{9,6},{10,7},{11,8},{12,9},{13... | collective-permute-start | bytes 1769480 | tf_op jit(solution)/shard_map/ppermute | solution.py:13
  529.8 44.7 %collective-permute-start.41 = (bf16[384,768]{1,0:T(8,128)(2,1)S(1)}, bf16[384,768]{1,0:T(8,128)(2,1)S(1)}, u32[]{:S(2)}, u32[]{:S(2)}) collective-permute-start(bf16[384,768]{1,0:T(8,128)(2,1)S(1)} %convolution_convert_fusion.1), channel_id=1, source_target_pairs={{4,0},{5,1},{6,2},{7,3},{8,4},{9,5},{10,6},{11,7},{12,8},{13,9},{1... | collective-permute-start | bytes 1769480 | tf_op jit(solution)/shard_map/ppermute | solution.py:13
  532.0 49.6 %collective-permute-start.42 = (bf16[384,768]{1,0:T(8,128)(2,1)S(1)}, bf16[384,768]{1,0:T(8,128)(2,1)S(1)}, u32[]{:S(2)}, u32[]{:S(2)}) collective-permute-start(bf16[384,768]{1,0:T(8,128)(2,1)S(1)} %convolution_convert_fusion.1), channel_id=1, source_target_pairs={{5,0},{6,1},{7,2},{8,3},{9,4},{10,5},{11,6},{12,7},{13,8},{14,9},{... | collective-permute-start | bytes 1769480 | tf_op jit(solution)/shard_map/ppermute | solution.py:13
  570.2 56.5 %collective-permute-start.44 = (bf16[384,768]{1,0:T(8,128)(2,1)S(1)}, bf16[384,768]{1,0:T(8,128)(2,1)S(1)}, u32[]{:S(2)}, u32[]{:S(2)}) collective-permute-start(bf16[384,768]{1,0:T(8,128)(2,1)S(1)} %convolution_convert_fusion.1), channel_id=1, source_target_pairs={{12,0},{13,1},{14,2},{15,3},{16,4},{17,5},{18,6},{19,7},{20,8},{21... | collective-permute-start | bytes 1769480 | tf_op jit(solution)/shard_map/ppermute | solution.py:13
  572.4 56.6 %collective-permute-start.45 = (bf16[384,768]{1,0:T(8,128)(2,1)S(1)}, bf16[384,768]{1,0:T(8,128)(2,1)S(1)}, u32[]{:S(2)}, u32[]{:S(2)}) collective-permute-start(bf16[384,768]{1,0:T(8,128)(2,1)S(1)} %convolution_convert_fusion.1), channel_id=1, source_target_pairs={{13,0},{14,1},{15,2},{16,3},{17,4},{18,5},{19,6},{20,7},{21,8},{22... | collective-permute-start | bytes 1769480 | tf_op jit(solution)/shard_map/ppermute | solution.py:13
  574.5 56.6 %collective-permute-start.46 = (bf16[384,768]{1,0:T(8,128)(2,1)S(1)}, bf16[384,768]{1,0:T(8,128)(2,1)S(1)}, u32[]{:S(2)}, u32[]{:S(2)}) collective-permute-start(bf16[384,768]{1,0:T(8,128)(2,1)S(1)} %convolution_convert_fusion.1), channel_id=1, source_target_pairs={{15,0},{16,1},{17,2},{18,3},{19,4},{20,5},{21,6},{22,7},{23,8},{24... | collective-permute-start | bytes 1769480 | tf_op jit(solution)/shard_map/ppermute | solution.py:13
  581.6 123.4 %collective-permute-start.47 = (bf16[384,768]{1,0:T(8,128)(2,1)S(1)}, bf16[384,768]{1,0:T(8,128)(2,1)S(1)}, u32[]{:S(2)}, u32[]{:S(2)}) collective-permute-start(bf16[384,768]{1,0:T(8,128)(2,1)S(1)} %convolution_convert_fusion.1), channel_id=1, source_target_pairs={{16,0},{17,1},{18,2},{19,3},{20,4},{21,5},{22,6},{23,7},{24,8},{25... | collective-permute-start | bytes 1769480 | tf_op jit(solution)/shard_map/ppermute | solution.py:13
  587.4 118.5 %collective-permute-start.48 = (bf16[384,768]{1,0:T(8,128)(2,1)S(1)}, bf16[384,768]{1,0:T(8,128)(2,1)S(1)}, u32[]{:S(2)}, u32[]{:S(2)}) collective-permute-start(bf16[384,768]{1,0:T(8,128)(2,1)S(1)} %convolution_convert_fusion.1), channel_id=1, source_target_pairs={{17,0},{18,1},{19,2},{20,3},{21,4},{22,5},{23,6},{24,7},{25,8},{26... | collective-permute-start | bytes 1769480 | tf_op jit(solution)/shard_map/ppermute | solution.py:13
  626.7 100.7 %collective-permute-start.49 = (bf16[384,768]{1,0:T(8,128)(2,1)S(1)}, bf16[384,768]{1,0:T(8,128)(2,1)S(1)}, u32[]{:S(2)}, u32[]{:S(2)}) collective-permute-start(bf16[384,768]{1,0:T(8,128)(2,1)S(1)} %convolution_convert_fusion.1), channel_id=1, source_target_pairs={{19,0},{20,1},{21,2},{22,3},{23,4},{24,5},{25,6},{26,7},{27,8},{28... | collective-permute-start | bytes 1769480 | tf_op jit(solution)/shard_map/ppermute | solution.py:13
  628.9 116.9 %collective-permute-start.50 = (bf16[384,768]{1,0:T(8,128)(2,1)S(1)}, bf16[384,768]{1,0:T(8,128)(2,1)S(1)}, u32[]{:S(2)}, u32[]{:S(2)}) collective-permute-start(bf16[384,768]{1,0:T(8,128)(2,1)S(1)} %convolution_convert_fusion.1), channel_id=1, source_target_pairs={{20,0},{21,1},{22,2},{23,3},{24,4},{25,5},{26,6},{27,7},{28,8},{29... | collective-permute-start | bytes 1769480 | tf_op jit(solution)/shard_map/ppermute | solution.py:13
  631.1 115.6 %collective-permute-start.51 = (bf16[384,768]{1,0:T(8,128)(2,1)S(1)}, bf16[384,768]{1,0:T(8,128)(2,1)S(1)}, u32[]{:S(2)}, u32[]{:S(2)}) collective-permute-start(bf16[384,768]{1,0:T(8,128)(2,1)S(1)} %convolution_convert_fusion.1), channel_id=1, source_target_pairs={{21,0},{22,1},{23,2},{24,3},{25,4},{26,5},{27,6},{28,7},{29,8},{30... | collective-permute-start | bytes 1769480 | tf_op jit(solution)/shard_map/ppermute | solution.py:13
  (12 other events, 234.7 us)
Sparse Core Ops, SparseCore 0:
  9.0 17.2 all-gather.1
  930.1 26.4 reduce-scatter.1
where the time goes:
time: 974 us; the launch traced here: 964 us
  waiting for transfers between devices  416 us (43%)
  starting transfers between devices  262 us (27%)
  matrix products  122 us (13%)
  local copies, waits for them, and re-layouts  79.7 us (8%)
  other arithmetic  69.4 us (7%)
  between operations  15.2 us (2%)
    ppermute x52, waiting for transfers between devices, passed_along(): return lax.ppermute(x, axis, pairs)  373 us
    ppermute x52, starting transfers between devices, passed_along(): return lax.ppermute(x, axis, pairs)  262 us
    dot_general x6, matrix products, on_device(): jnp.dot(expo.astype(jnp.bfloat16), chosen_v[:, cols], preferred_element_t...  51.8 us
    unnamed x64, local copies, waits for them, and re-layouts  50.5 us
    dot_general x6, matrix products, on_device(): lax.dot_general(queries[:, cols], chosen_k[:, cols], (((1,), (1,)), ((),...  50.1 us
    reduce_sum x6, other arithmetic, on_device(): total = jnp.sum(expo, axis=-1)  47 us
    reduce_scatter x1, waiting for transfers between devices, on_device(): lax.psum_scatter(partial_out.astype(jnp.bfloat16), 'heads', scatter_dimen...  26.6 us
  transfers between devices with their start and end apart: 54, of which 21 were waited for; matrix products, arithmetic and copies ran while one was open for 8% of the time, Pallas kernels for 0%

commit v1 on v0

v1 whole, which is shorter than its diff:
```python
import functools
import math

import jax
import jax.numpy as jnp
from jax import lax
from jax.experimental import pallas as pl
from jax.experimental.pallas import tpu as pltpu
from jax.sharding import PartitionSpec as P

MESH = pl.DeviceIdType.MESH
GRID = 4
NEG = -1e30
FLOOR = -1e20
CENTRE = 21
TABLE = 48
BF16 = jnp.bfloat16
F32 = jnp.float32
NT = (((1,), (1,)), ((), ()))


def stride_of(axis):
    return 16 + (9 * axis * axis - 33 * axis) // 2


def neighbour(me, axis, by):
    stride = stride_of(axis)
    place = (me // stride) % GRID
    return me + ((place + by + GRID) % GRID - place) * stride


def kernel(
    blocks,
    x_hbm, wq_hbm, wk_hbm, wv_hbm, wo_hbm, qg_ref, kg_ref, ids_ref, cnt_ref,
    out_ref,
    xbuf, wbuf, wobuf, kbuf, vbuf, qbuf, acc, top, tot, osend, orecv, ssend, srecv, attbuf, table,
    load_sem, pair_send, pair_recv, tab_send, tab_recv,
    own_send, fwd_send, kv_recv, q_send, q_recv, o_send, o_recv,
):
    me = lax.axis_index("seq")
    half = lax.axis_index("heads")
    tile = x_hbm.shape[0]
    cols = x_hbm.shape[1]
    hd = qg_ref.shape[1]
    group = wq_hbm.shape[1] // hd
    hg = group // 2
    scale = math.log2(math.e) / math.sqrt(hd)

    def remote(src, dst, send, recv, device):
        return pltpu.make_async_remote_copy(
            src_ref=src, dst_ref=dst, send_sem=send, recv_sem=recv, device_id=device, device_id_type=MESH
        )

    loads = [pltpu.make_async_copy(x_hbm, xbuf.at[half], load_sem.at[0])]
    for pair in range(hg):
        for kind, ref in enumerate((wk_hbm, wv_hbm, wq_hbm)):
            loads.append(
                pltpu.make_async_copy(
                    ref.at[:, 2 * hd * pair : 2 * hd * (pair + 1)],
                    wbuf.at[kind, pair],
                    load_sem.at[1 + 3 * pair + kind],
                )
            )
    wo_own = pltpu.make_async_copy(
        wo_hbm.at[:, pl.ds(pl.multiple_of(half * cols, cols), cols)], wobuf.at[half], load_sem.at[1 + 3 * hg]
    )
    for copy in loads:
        copy.start()

    partner = (1 - half, me)
    barrier = pltpu.get_barrier_semaphore()
    for axis in range(3):
        for by in (1, -1):
            pl.semaphore_signal(barrier, inc=1, device_id=(half, neighbour(me, axis, by)), device_id_type=MESH)
    pl.semaphore_signal(barrier, inc=1, device_id=partner, device_id_type=MESH)
    pl.semaphore_wait(barrier, 7)

    x_copy = remote(x_hbm, xbuf.at[half], pair_send.at[0], pair_recv.at[0], partner)
    x_copy.start()
    wo_copy = remote(
        wo_hbm.at[:, pl.ds(pl.multiple_of((1 - half) * cols, cols), cols)],
        wobuf.at[half], pair_send.at[1], pair_recv.at[1], partner,
    )

    ids = ids_ref[...]
    used = lax.broadcasted_iota(jnp.int32, ids.shape, 1) < cnt_ref[...]
    wanted = lax.broadcasted_iota(jnp.int32, (TABLE, 1), 0) + (me - CENTRE)
    hit = jnp.where((ids == wanted) & used, 0.0, NEG)
    table[0] = jnp.broadcast_to(jnp.max(hit, axis=1, keepdims=True), (TABLE, hd))
    tab_copies = []
    for axis in range(3):
        for e, by in enumerate((1, -1)):
            tab_copies.append(
                remote(
                    table.at[0], table.at[2 + 2 * axis - e], tab_send.at[2 * axis + e],
                    tab_recv.at[2 * axis + 1 - e], (half, neighbour(me, axis, by)),
                )
            )
    for copy in tab_copies:
        copy.start()

    def kv_dst(h, grp, e):
        return kbuf.at[h, grp, pl.ds(e * tile, tile)], vbuf.at[h, grp, :, e * tile : (e + 1) * tile]

    def own_copies(h):
        o = h % 3
        out = []
        for role, grp in ((1, 1), (2, 2)):
            for e, by in enumerate((1, -1)):
                device = (half, neighbour(me, (o + role) % 3, by))
                for kv in range(2):
                    out.append(
                        remote(
                            kv_dst(h, 0, 0)[kv], kv_dst(h, grp, 1 - e)[kv], own_send.at[h, 2 * grp - 2 + e, kv],
                            kv_recv.at[h, grp, 1 - e, kv], device,
                        )
                    )
        return out

    def fwd_copies(h):
        o = h % 3
        out = []
        for b in range(2):
            for e, by in enumerate((1, -1)):
                device = (half, neighbour(me, (o + 2) % 3, by))
                for kv in range(2):
                    out.append(
                        remote(
                            kv_dst(h, 1, b)[kv], kv_dst(h, 3 + b, 1 - e)[kv], fwd_send.at[h, 2 * b + e, kv],
                            kv_recv.at[h, 3 + b, 1 - e, kv], device,
                        )
                    )
        return out

    def q_copies(h):
        return [
            remote(
                qbuf.at[h, 0:tile], qbuf.at[h, (2 - e) * tile : (3 - e) * tile], q_send.at[h, e],
                q_recv.at[h, 1 - e], (half, neighbour(me, h % 3, by)),
            )
            for e, by in enumerate((1, -1))
        ]

    def o_copies(h):
        out = []
        for e, by in enumerate((1, -1)):
            device = (half, neighbour(me, h % 3, by))
            out.append(remote(osend.at[h, e], orecv.at[h, 1 - e], o_send.at[h, e, 0], o_recv.at[h, 1 - e, 0], device))
            out.append(remote(ssend.at[h, e], srecv.at[h, 1 - e], o_send.at[h, e, 1], o_recv.at[h, 1 - e, 1], device))
        return out

    def start(copies):
        for copy in copies:
            copy.start()

    loads[0].wait()
    x_copy.wait_recv()

    def project(kind, pair):
        total = jnp.dot(xbuf[0], wbuf[kind, pair, :cols], preferred_element_type=F32)
        return total + jnp.dot(xbuf[1], wbuf[kind, pair, cols:], preferred_element_type=F32)

    def normal(rows, gain):
        meansq = jnp.mean(rows * rows, axis=-1, keepdims=True)
        return (rows * lax.rsqrt(meansq + 1e-06) * gain).astype(BF16)

    def one_pair(pair, carry):
        for kind, ref in enumerate((wk_hbm, wv_hbm)):
            pltpu.make_async_copy(
                ref.at[:, 0 : 2 * hd], wbuf.at[kind, pair], load_sem.at[1 + 3 * pair + kind]
            ).wait()
        proj = project(0, pair)
        for e in range(2):
            kbuf[2 * pair + e, 0, 0:tile, :] = normal(proj[:, e * hd : (e + 1) * hd], kg_ref[...])
        proj = project(1, pair)
        for e in range(2):
            vbuf[2 * pair + e, 0, :, 0:tile] = jnp.transpose(proj[:, e * hd : (e + 1) * hd]).astype(BF16)
        for e in range(2):
            start(own_copies(2 * pair + e))
        pltpu.make_async_copy(wq_hbm.at[:, 0 : 2 * hd], wbuf.at[2, pair], load_sem.at[3 + 3 * pair]).wait()
        proj = project(2, pair)
        for e in range(2):
            qbuf[2 * pair + e, 0:tile, :] = normal(proj[:, e * hd : (e + 1) * hd], qg_ref[...])
        for e in range(2):
            start(q_copies(2 * pair + e))
        return carry

    lax.fori_loop(0, hg, one_pair, 0)
    wo_own.start()
    wo_copy.start()
    for copy in tab_copies:
        copy.wait_recv()

    def shifts(h, b, g):
        o = h % 3
        sa, sb, sg = stride_of(o), stride_of((o + 1) % 3), stride_of((o + 2) % 3)
        parts = []
        for which, a in ((0, 0), (1, 1), (2, -1)):
            row = CENTRE - a * sa + b * sb + g * sg
            slot = 0 if which == 0 else 2 * o + which
            parts += [table[slot, pl.ds(row, 1), :]] * (tile // hd)
        return jnp.concatenate(parts, axis=1)

    def attend(h, grp, size, bias, first):
        keys = len(bias) * size
        wide = [slice(c, c + w) for c, w in blocks]

        def scores(cl):
            return lax.dot_general(kbuf[h, grp, 0:keys, :], qbuf[h, cl, :], NT, preferred_element_type=F32)

        def weigh(s, cl):
            parts = [s[t * size : (t + 1) * size] for t in range(len(bias))]
            new = jnp.full((1, s.shape[1]), FLOOR, F32) if first else top[h, 0:1, cl]
            old = new
            for part, shift in zip(parts, bias):
                new = jnp.maximum(new, jnp.max(part, axis=0, keepdims=True) + shift[:, cl])
            expo = [jnp.exp2(part * scale - (new - shift[:, cl]) * scale) for part, shift in zip(parts, bias)]
            sums = sum(jnp.sum(part, axis=0, keepdims=True) for part in expo)
            keep = None
            if not first:
                keep = jnp.exp2((old - new) * scale)
                sums = sums + tot[h, 0:1, cl] * keep
            tot[h, 0:1, cl] = sums
            top[h, 0:1, cl] = new
            return keep, jnp.concatenate([part.astype(BF16) for part in expo], axis=0)

        def add(keep, weight, cl):
            new = jnp.dot(vbuf[h, grp, :, 0:keys], weight, preferred_element_type=F32)
            acc[h, :, cl] = new if first else acc[h, :, cl] * keep + new

        s = scores(wide[0])
        for n, cl in enumerate(wide):
            later = scores(wide[n + 1]) if n + 1 < len(wide) else None
            keep, weight = weigh(s, cl)
            add(keep, weight, cl)
            s = later

    def own_step(h, carry):
        for copy in q_copies(h):
            copy.wait_recv()
        attend(h, 0, tile, [shifts(h, 0, 0)], True)
        return carry

    lax.fori_loop(0, group, own_step, 0)

    def step(t, carry):
        block, rest = t // 3, t % 3
        h = 3 * ((block // 2) % 2) + rest
        grp = 1 + block % 2 + 2 * (block // 4)
        for e in range(2):
            for kv in range(2):
                dst = kv_dst(h, grp, e)[kv]
                remote(dst, dst, own_send.at[h, 0, kv], kv_recv.at[h, grp, e, kv], partner).wait_recv()

        @pl.when(grp == 1)
        def _():
            start(fwd_copies(h))

        late = block // 4
        odd = block % 2
        b0 = late * (1 - 2 * odd) + (1 - late) * (1 - odd)
        b1 = late * (1 - 2 * odd) - (1 - late) * (1 - odd)
        g0 = late + (1 - late) * odd
        attend(h, grp, tile, [shifts(h, b0, g0), shifts(h, b1, 0 - g0)], False)

        @pl.when(grp == 4)
        def _():
            for e in range(2):
                cl = slice((1 + e) * tile, (2 + e) * tile)
                osend[h, e] = acc[h, :, cl].astype(BF16)
                ssend[h, e, 0:1, :] = top[h, 0:1, cl]
                ssend[h, e, 1:2, :] = tot[h, 0:1, cl]
            start(o_copies(h))

        return carry

    lax.fori_loop(0, 24, step, 0)

    def combine(h, carry):
        for copy in o_copies(h):
            copy.wait_recv()
        tops = [top[h, 0:1, 0:tile], srecv[h, 0, 0:1, :], srecv[h, 1, 0:1, :]]
        tots = [tot[h, 0:1, 0:tile], srecv[h, 0, 1:2, :], srecv[h, 1, 1:2, :]]
        high = jnp.maximum(tops[0], jnp.maximum(tops[1], tops[2]))
        share = [jnp.exp2((each - high) * scale) for each in tops]
        total = share[0] * tots[0] + share[1] * tots[1] + share[2] * tots[2]
        summed = acc[h, :, 0:tile] * share[0]
        for e in range(2):
            summed = summed + orecv[h, e].astype(F32) * share[1 + e]
        att = jnp.transpose(summed / total).astype(BF16)
        attbuf[half, :, pl.ds(pl.multiple_of(h * hd, hd), hd)] = att
        return carry

    lax.fori_loop(0, group, combine, 0)
    att_copy = remote(attbuf.at[half], attbuf.at[half], pair_send.at[2], pair_recv.at[2], partner)
    att_copy.start()
    wo_own.wait()
    wo_copy.wait_recv()
    att_copy.wait_recv()

    width = 2 * hd

    def project_out(c, carry):
        span = pl.ds(pl.multiple_of(c * width, width), width)
        total = jnp.dot(attbuf[0], wobuf[0, :, span], preferred_element_type=F32)
        total = total + jnp.dot(attbuf[1], wobuf[1, :, span], preferred_element_type=F32)
        out_ref[:, span] = total.astype(BF16)
        return carry

    lax.fori_loop(0, cols // width, project_out, 0)

    x_copy.wait_send()
    wo_copy.wait_send()
    att_copy.wait_send()
    for copy in tab_copies:
        copy.wait_send()

    def drain(h, carry):
        for copy in own_copies(h) + fwd_copies(h) + q_copies(h) + o_copies(h):
            copy.wait_send()
        return carry

    lax.fori_loop(0, group, drain, 0)


def on_device(blocks, tokens, w_query, w_key, w_value, query_gain, key_gain, w_out, key_tiles, key_counts):
    tile, cols = tokens.shape
    hd = query_gain.shape[0]
    heads = w_query.shape[1]
    group = heads // hd
    hg = group // 2
    any_space = pl.BlockSpec(memory_space=pl.ANY)
    vmem = pl.BlockSpec(memory_space=pltpu.VMEM)
    dma = pltpu.SemaphoreType.DMA
    return pl.pallas_call(
        functools.partial(kernel, blocks),
        out_shape=jax.ShapeDtypeStruct((tile, cols), BF16),
        in_specs=[any_space] * 5 + [vmem] * 4,
        out_specs=vmem,
        scratch_shapes=[
            pltpu.VMEM((2, tile, cols), BF16),
            pltpu.VMEM((3, hg, 2 * cols, 2 * hd), BF16),
            pltpu.VMEM((2, heads, cols), BF16),
            pltpu.VMEM((group, 5, 2 * tile, hd), BF16),
            pltpu.VMEM((group, 5, hd, 2 * tile), BF16),
            pltpu.VMEM((group, 3 * tile, hd), BF16),
            pltpu.VMEM((group, hd, 3 * tile), F32),
            pltpu.VMEM((group, 8, 3 * tile), F32),
            pltpu.VMEM((group, 8, 3 * tile), F32),
            pltpu.VMEM((group, 2, hd, tile), BF16),
            pltpu.VMEM((group, 2, hd, tile), BF16),
            pltpu.VMEM((group, 2, 8, tile), F32),
            pltpu.VMEM((group, 2, 8, tile), F32),
            pltpu.VMEM((2, tile, heads), BF16),
            pltpu.VMEM((7, TABLE, hd), F32),
            dma((2 + 3 * hg,)),
            dma((3,)),
            dma((3,)),
            dma((6,)),
            dma((6,)),
            dma((group, 4, 2)),
            dma((group, 4, 2)),
            dma((group, 5, 2, 2)),
            dma((group, 2)),
            dma((group, 2)),
            dma((group, 2, 2)),
            dma((group, 2, 2)),
        ],
        compiler_params=pltpu.CompilerParams(collective_id=0, has_side_effects=True, vmem_limit_bytes=66 * 2**20 - 2**21),
        name="tile_attention",
    )(
        tokens, w_query, w_key, w_value, w_out,
        query_gain.reshape(1, hd), key_gain.reshape(1, hd), key_tiles, key_counts.reshape(1, 1),
    )


BLOCKS = tuple((c * 128, 128) for c in range(9))


def solution(mesh):
    return jax.shard_map(
        functools.partial(on_device, BLOCKS),
        mesh=mesh,
        in_specs=(
            P("seq", "heads"),
            P(None, "heads"),
            P(None, "heads"),
            P(None, "heads"),
            P(),
            P(),
            P("heads", None),
            P("seq", None),
            P("seq"),
        ),
        out_specs=P("seq", "heads"),
        check_vma=False,
    )
```

time: 974 us -> 97.1 us (0.10); the launches traced: 964 us -> 96.9 us
  waiting for transfers between devices: 416 us -> 0 us
  starting transfers between devices: 262 us -> 0 us
  matrix products: 122 us -> 0 us
  Pallas kernels: 0 us -> 93.9 us
  local copies, waits for them, and re-layouts: 79.7 us -> 2.36 us
  other arithmetic: 69.4 us -> 0 us
  between operations: 15.2 us -> 0.66 us
    ppermute x52 -> x0, waiting for transfers between devices: 373 us -> none  [passed_along(): return lax.ppermute(x, axis, pairs)]
    ppermute x52 -> x0, starting transfers between devices: 262 us -> none  [passed_along(): return lax.ppermute(x, axis, pairs)]
    dot_general x16 -> x0, matrix products: 122 us -> none  [the longest x6 51.8 us: on_device(): jnp.dot(expo.astype(jnp.bfloat16), chosen_v[:, cols], preferred_element_t...]
    pallas_call x0 -> x1, Pallas kernels: none -> 93.9 us  [on_device(): pl.pallas_call(functools.partial(kernel, blocks), out_shape=jax.ShapeDtyp...]
    unnamed x64 -> x1, local copies, waits for them, and re-layouts: 50.5 us -> 2.36 us
    reduce_sum x8 -> x0, other arithmetic: 47.1 us -> none  [the longest x6 47 us: on_device(): total = jnp.sum(expo, axis=-1)]
    reduce_scatter x1 -> x0, waiting for transfers between devices: 26.6 us -> none  [on_device(): lax.psum_scatter(partial_out.astype(jnp.bfloat16), 'heads', scatter_dimen...]
    gather x2 -> x0, local copies, waits for them, and re-layouts: 25.2 us -> none  [the longest x1 12.7 us: on_device(): jnp.take(stack_v, codes, axis=0).reshape(slots * tile_rows, width)]
  transfers between devices with their start and end apart: 54 -> 0, of which waited for: 21 -> 0; matrix products, arithmetic and copies ran while one was open for 8% -> 0% of each run, Pallas kernels for 0% -> 0%
where the time goes in v1:
time: 97.1 us; the launch traced here: 96.9 us
  Pallas kernels  93.9 us (97%)
  local copies, waits for them, and re-layouts  2.36 us (2%)
    pallas_call x1, Pallas kernels, on_device(): pl.pallas_call(functools.partial(kernel, blocks), out_shape=jax.ShapeDtyp...  93.9 us
    unnamed x1, local copies, waits for them, and re-layouts  2.36 us

profile of v1, /device:TPU:1, one launch (start us, length us, event | category | flops | bytes accessed | tf_op | source)
XLA Modules:
  0.0 96.9 jit_solution(18118583593969067729)
XLA Ops:
  0.7 93.9 %tile_attention.1 = bf16[384,1536]{1,0:T(8,128)(2,1)} custom-call(bf16[384,1536]{1,0:T(8,128)(2,1)} %x_hbm.1, bf16[3072,768]{1,0:T(8,128)(2,1)} %wq_hbm.1, bf16[3072,768]{1,0:T(8,128)(2,1)} %wk_hbm.1, bf16[3072,768]{1,0:T(8,128)(2,1)} %wv_hbm.1, bf16[768,3072]{1,0:T(8,128)(2,1)} %wo_hbm.1, f32[1,128]{1,0:T(1,128)} %bitcast.4, f32[1,128]{1,0:T(1,128)} %bitcast.5, ...), custom_call_target="tpu_custom_call" | custom-call | tf_op jit(solution)/shard_map/tile_attention/pallas_call | solution.py:335
  94.6 2.4 %copy.12 = bf16[384,1536]{1,0:T(8,128)(2,1)} copy(bf16[384,1536]{1,0:T(8,128)(2,1)} %tile_attention.1) | data formatting | bytes 2359296

commit v2 on v1

--- a/solution.py
+++ b/solution.py
@@ -33,7 +33,7 @@
     blocks,
     x_hbm, wq_hbm, wk_hbm, wv_hbm, wo_hbm, qg_ref, kg_ref, ids_ref, cnt_ref,
     out_ref,
-    xbuf, wbuf, wobuf, kbuf, vbuf, qbuf, acc, top, tot, osend, orecv, ssend, srecv, attbuf, table,
+    xbuf, wbuf, wobuf, kbuf, vbuf, qbuf, acc, top, tot, osend, orecv, ssend, srecv, attbuf, table, partial, outacc,
     load_sem, pair_send, pair_recv, tab_send, tab_recv,
     own_send, fwd_send, kv_recv, q_send, q_recv, o_send, o_recv,
 ):
@@ -61,9 +61,13 @@
                     load_sem.at[1 + 3 * pair + kind],
                 )
             )
-    wo_own = pltpu.make_async_copy(
-        wo_hbm.at[:, pl.ds(pl.multiple_of(half * cols, cols), cols)], wobuf.at[half], load_sem.at[1 + 3 * hg]
-    )
+    part = hg * hd
+
+    def wo_slices(wave, side):
+        src = wo_hbm.at[wave * part : (wave + 1) * part, pl.ds(pl.multiple_of(side * cols, cols), cols)]
+        return src, wobuf.at[wave, pl.ds(pl.multiple_of(half * part, part), part)]
+
+    wo_own = [pltpu.make_async_copy(*wo_slices(wave, half), load_sem.at[1 + 3 * hg + wave]) for wave in range(2)]
     for copy in loads:
         copy.start()
 
@@ -77,10 +81,9 @@
 
     x_copy = remote(x_hbm, xbuf.at[half], pair_send.at[0], pair_recv.at[0], partner)
     x_copy.start()
-    wo_copy = remote(
-        wo_hbm.at[:, pl.ds(pl.multiple_of((1 - half) * cols, cols), cols)],
-        wobuf.at[half], pair_send.at[1], pair_recv.at[1], partner,
-    )
+    wo_copy = [
+        remote(*wo_slices(wave, 1 - half), pair_send.at[1 + wave], pair_recv.at[1 + wave], partner) for wave in range(2)
+    ]
 
     ids = ids_ref[...]
     used = lax.broadcasted_iota(jnp.int32, ids.shape, 1) < cnt_ref[...]
@@ -154,21 +157,32 @@
             copy.start()
 
     loads[0].wait()
+
+    def own_half(pair, carry):
+        for kind, ref in ((2, wq_hbm), (0, wk_hbm), (1, wv_hbm)):
+            pltpu.make_async_copy(
+                ref.at[:, 0 : 2 * hd], wbuf.at[kind, pair], load_sem.at[1 + 3 * pair + kind]
+            ).wait()
+        rows = pl.ds(pl.multiple_of(half * cols, cols), cols)
+        for kind in (2, 0, 1):
+            partial[kind, pair] = jnp.dot(xbuf[half], wbuf[kind, pair, rows], preferred_element_type=F32)
+        return carry
+
+    lax.fori_loop(0, hg, own_half, 0)
     x_copy.wait_recv()
 
     def project(kind, pair):
-        total = jnp.dot(xbuf[0], wbuf[kind, pair, :cols], preferred_element_type=F32)
-        return total + jnp.dot(xbuf[1], wbuf[kind, pair, cols:], preferred_element_type=F32)
+        rows = pl.ds(pl.multiple_of((1 - half) * cols, cols), cols)
+        return partial[kind, pair] + jnp.dot(xbuf[1 - half], wbuf[kind, pair, rows], preferred_element_type=F32)
 
     def normal(rows, gain):
         meansq = jnp.mean(rows * rows, axis=-1, keepdims=True)
         return (rows * lax.rsqrt(meansq + 1e-06) * gain).astype(BF16)
 
     def one_pair(pair, carry):
-        for kind, ref in enumerate((wk_hbm, wv_hbm)):
-            pltpu.make_async_copy(
-                ref.at[:, 0 : 2 * hd], wbuf.at[kind, pair], load_sem.at[1 + 3 * pair + kind]
-            ).wait()
+        proj = project(2, pair)
+        for e in range(2):
+            qbuf[2 * pair + e, 0:tile, :] = normal(proj[:, e * hd : (e + 1) * hd], qg_ref[...])
         proj = project(0, pair)
         for e in range(2):
             kbuf[2 * pair + e, 0, 0:tile, :] = normal(proj[:, e * hd : (e + 1) * hd], kg_ref[...])
@@ -176,18 +190,14 @@
         for e in range(2):
             vbuf[2 * pair + e, 0, :, 0:tile] = jnp.transpose(proj[:, e * hd : (e + 1) * hd]).astype(BF16)
         for e in range(2):
+            start(q_copies(2 * pair + e))
+        for e in range(2):
             start(own_copies(2 * pair + e))
-        pltpu.make_async_copy(wq_hbm.at[:, 0 : 2 * hd], wbuf.at[2, pair], load_sem.at[3 + 3 * pair]).wait()
-        proj = project(2, pair)
-        for e in range(2):
-            qbuf[2 * pair + e, 0:tile, :] = normal(proj[:, e * hd : (e + 1) * hd], qg_ref[...])
-        for e in range(2):
-            start(q_copies(2 * pair + e))
         return carry
 
     lax.fori_loop(0, hg, one_pair, 0)
-    wo_own.start()
-    wo_copy.start()
+    start(wo_own)
+    start(wo_copy)
     for copy in tab_copies:
         copy.wait_recv()
 
@@ -201,9 +211,9 @@
             parts += [table[slot, pl.ds(row, 1), :]] * (tile // hd)
         return jnp.concatenate(parts, axis=1)
 
-    def attend(h, grp, size, bias, first):
+    def attend(h, grp, size, bias, first, slots=(0, 1, 2)):
         keys = len(bias) * size
-        wide = [slice(c, c + w) for c, w in blocks]
+        wide = [slice(c, c + w) for c, w in blocks if c // tile in slots]
 
         def scores(cl):
             return lax.dot_general(kbuf[h, grp, 0:keys, :], qbuf[h, cl, :], NT, preferred_element_type=F32)
@@ -241,40 +251,66 @@
         attend(h, 0, tile, [shifts(h, 0, 0)], True)
         return carry
 
-    lax.fori_loop(0, group, own_step, 0)
-
-    def step(t, carry):
-        block, rest = t // 3, t % 3
-        h = 3 * ((block // 2) % 2) + rest
-        grp = 1 + block % 2 + 2 * (block // 4)
+    lax.fori_loop(0, hg, own_step, 0)
+
+    def place(t):
+        block = t // 3
+        return 3 * ((block // 2) % 2) + t % 3, 1 + block % 2 + 2 * (block // 4)
+
+    def group_bias(h, t):
+        block = t // 3
+        late, odd = block // 4, block % 2
+        b0 = late * (1 - 2 * odd) + (1 - late) * (1 - odd)
+        b1 = late * (1 - 2 * odd) - (1 - late) * (1 - odd)
+        g0 = late + (1 - late) * odd
+        return [shifts(h, b0, g0), shifts(h, b1, 0 - g0)]
+
+    def arrive(h, grp):
         for e in range(2):
             for kv in range(2):
                 dst = kv_dst(h, grp, e)[kv]
                 remote(dst, dst, own_send.at[h, 0, kv], kv_recv.at[h, grp, e, kv], partner).wait_recv()
 
+    def give_back(h):
+        for e in range(2):
+            cl = slice((1 + e) * tile, (2 + e) * tile)
+            osend[h, e] = acc[h, :, cl].astype(BF16)
+            ssend[h, e, 0:1, :] = top[h, 0:1, cl]
+            ssend[h, e, 1:2, :] = tot[h, 0:1, cl]
+        start(o_copies(h))
+
+    def step(t, carry):
+        h, grp = place(t)
+
+        @pl.when(t // 3 == 2)
+        def _():
+            own_step(h, 0)
+
+        arrive(h, grp)
+
         @pl.when(grp == 1)
         def _():
             start(fwd_copies(h))
 
-        late = block // 4
-        odd = block % 2
-        b0 = late * (1 - 2 * odd) + (1 - late) * (1 - odd)
-        b1 = late * (1 - 2 * odd) - (1 - late) * (1 - odd)
-        g0 = late + (1 - late) * odd
-        attend(h, grp, tile, [shifts(h, b0, g0), shifts(h, b1, 0 - g0)], False)
+        attend(h, grp, tile, group_bias(h, t), False)
 
         @pl.when(grp == 4)
         def _():
-            for e in range(2):
-                cl = slice((1 + e) * tile, (2 + e) * tile)
-                osend[h, e] = acc[h, :, cl].astype(BF16)
-                ssend[h, e, 0:1, :] = top[h, 0:1, cl]
-                ssend[h, e, 1:2, :] = tot[h, 0:1, cl]
-            start(o_copies(h))
-
-        return carry
-
-    lax.fori_loop(0, 24, step, 0)
+            give_back(h)
+
+        return carry
+
+    def last_others(t, carry):
+        h, grp = place(t)
+        arrive(h, grp)
+        attend(h, grp, tile, group_bias(h, t), False, (1, 2))
+        give_back(h)
+        return carry
+
+    def last_own(t, carry):
+        h, grp = place(t)
+        attend(h, grp, tile, group_bias(h, t), False, (0,))
+        return carry
 
     def combine(h, carry):
         for copy in o_copies(h):
@@ -288,31 +324,48 @@
         for e in range(2):
             summed = summed + orecv[h, e].astype(F32) * share[1 + e]
         att = jnp.transpose(summed / total).astype(BF16)
-        attbuf[half, :, pl.ds(pl.multiple_of(h * hd, hd), hd)] = att
-        return carry
-
-    lax.fori_loop(0, group, combine, 0)
-    att_copy = remote(attbuf.at[half], attbuf.at[half], pair_send.at[2], pair_recv.at[2], partner)
-    att_copy.start()
-    wo_own.wait()
-    wo_copy.wait_recv()
-    att_copy.wait_recv()
+        attbuf[h // 3, half, :, pl.ds(pl.multiple_of((h % 3) * hd, hd), hd)] = att
+        return carry
 
     width = 2 * hd
-
-    def project_out(c, carry):
+    att_copies = [
+        remote(attbuf.at[wave, half], attbuf.at[wave, half], pair_send.at[3 + wave], pair_recv.at[3 + wave], partner)
+        for wave in range(2)
+    ]
+
+    def project_out(wave, c):
         span = pl.ds(pl.multiple_of(c * width, width), width)
-        total = jnp.dot(attbuf[0], wobuf[0, :, span], preferred_element_type=F32)
-        total = total + jnp.dot(attbuf[1], wobuf[1, :, span], preferred_element_type=F32)
-        out_ref[:, span] = total.astype(BF16)
-        return carry
-
-    lax.fori_loop(0, cols // width, project_out, 0)
+        total = jnp.dot(attbuf[wave, 0], wobuf[wave, 0:part, span], preferred_element_type=F32)
+        return span, total + jnp.dot(attbuf[wave, 1], wobuf[wave, part:, span], preferred_element_type=F32)
+
+    def out_first(c, carry):
+        span, total = project_out(0, c)
+        outacc[:, span] = total
+        return carry
+
+    def out_second(c, carry):
+        span, total = project_out(1, c)
+        out_ref[:, span] = (outacc[:, span] + total).astype(BF16)
+        return carry
+
+    lax.fori_loop(0, 21, step, 0)
+    lax.fori_loop(21, 24, last_others, 0)
+    lax.fori_loop(0, hg, combine, 0)
+    att_copies[0].start()
+    lax.fori_loop(21, 24, last_own, 0)
+    for copy in wo_own:
+        copy.wait()
+    for copy in wo_copy:
+        copy.wait_recv()
+    att_copies[0].wait_recv()
+    lax.fori_loop(0, cols // width, out_first, 0)
+    lax.fori_loop(hg, group, combine, 0)
+    att_copies[1].start()
+    att_copies[1].wait_recv()
+    lax.fori_loop(0, cols // width, out_second, 0)
 
     x_copy.wait_send()
-    wo_copy.wait_send()
-    att_copy.wait_send()
-    for copy in tab_copies:
+    for copy in wo_copy + att_copies + tab_copies:
         copy.wait_send()
 
     def drain(h, carry):
@@ -351,11 +404,13 @@
             pltpu.VMEM((group, 2, hd, tile), BF16),
             pltpu.VMEM((group, 2, 8, tile), F32),
             pltpu.VMEM((group, 2, 8, tile), F32),
-            pltpu.VMEM((2, tile, heads), BF16),
+            pltpu.VMEM((2, 2, tile, hg * hd), BF16),
             pltpu.VMEM((7, TABLE, hd), F32),
-            dma((2 + 3 * hg,)),
-            dma((3,)),
-            dma((3,)),
+            pltpu.VMEM((3, hg, tile, 2 * hd), F32),
+            pltpu.VMEM((tile, cols), F32),
+            dma((3 + 3 * hg,)),
+            dma((5,)),
+            dma((5,)),
             dma((6,)),
             dma((6,)),
             dma((group, 4, 2)),

time: 97.1 us -> 86.7 us (0.89)
  Pallas kernels: 93.9 us -> 83.5 us
    pallas_call x1, Pallas kernels: 93.9 us -> 83.5 us  [on_device(): pl.pallas_call(functools.partial(kernel, blocks), out_shape=jax.ShapeDtyp...]
where the time goes in v2:
time: 86.7 us; the launch traced here: 86.6 us
  Pallas kernels  83.5 us (96%)
  local copies, waits for them, and re-layouts  2.36 us (3%)
    pallas_call x1, Pallas kernels, on_device(): pl.pallas_call(functools.partial(kernel, blocks), out_shape=jax.ShapeDtyp...  83.5 us
    unnamed x1, local copies, waits for them, and re-layouts  2.36 us

profile of v2, /device:TPU:1, one launch (start us, length us, event | category | flops | bytes accessed | tf_op | source)
XLA Modules:
  0.0 86.6 jit_solution(15512578217370370207)
XLA Ops:
  0.7 83.5 %tile_attention.1 = bf16[384,1536]{1,0:T(8,128)(2,1)} custom-call(bf16[384,1536]{1,0:T(8,128)(2,1)} %x_hbm.1, bf16[3072,768]{1,0:T(8,128)(2,1)} %wq_hbm.1, bf16[3072,768]{1,0:T(8,128)(2,1)} %wk_hbm.1, bf16[3072,768]{1,0:T(8,128)(2,1)} %wv_hbm.1, bf16[768,3072]{1,0:T(8,128)(2,1)} %wo_hbm.1, f32[1,128]{1,0:T(1,128)} %bitcast.4, f32[1,128]{1,0:T(1,128)} %bitcast.5, ...), custom_call_target="tpu_custom_call" | custom-call | tf_op jit(solution)/shard_map/tile_attention/pallas_call | solution.py:388
  84.2 2.4 %copy.12 = bf16[384,1536]{1,0:T(8,128)(2,1)} copy(bf16[384,1536]{1,0:T(8,128)(2,1)} %tile_attention.1) | data formatting | bytes 2359296

commit v3 on v2

--- a/solution.py
+++ b/solution.py
@@ -33,7 +33,7 @@
     blocks,
     x_hbm, wq_hbm, wk_hbm, wv_hbm, wo_hbm, qg_ref, kg_ref, ids_ref, cnt_ref,
     out_ref,
-    xbuf, wbuf, wobuf, kbuf, vbuf, qbuf, acc, top, tot, osend, orecv, ssend, srecv, attbuf, table, partial, outacc,
+    xbuf, wbuf, wobuf, kbuf, vbuf, qbuf, acc, top, tot, osend, orecv, ssend, srecv, attbuf, table, partial, outacc, pbuf,
     load_sem, pair_send, pair_recv, tab_send, tab_recv,
     own_send, fwd_send, kv_recv, q_send, q_recv, o_send, o_recv,
 ):
@@ -105,10 +105,11 @@
     def kv_dst(h, grp, e):
         return kbuf.at[h, grp, pl.ds(e * tile, tile)], vbuf.at[h, grp, :, e * tile : (e + 1) * tile]
 
-    def own_copies(h):
+    def own_copies(h, roles=(1, 2)):
         o = h % 3
         out = []
-        for role, grp in ((1, 1), (2, 2)):
+        for role in roles:
+            grp = role
             for e, by in enumerate((1, -1)):
                 device = (half, neighbour(me, (o + role) % 3, by))
                 for kv in range(2):
@@ -190,9 +191,11 @@
         for e in range(2):
             vbuf[2 * pair + e, 0, :, 0:tile] = jnp.transpose(proj[:, e * hd : (e + 1) * hd]).astype(BF16)
         for e in range(2):
-            start(q_copies(2 * pair + e))
-        for e in range(2):
-            start(own_copies(2 * pair + e))
+
+            @pl.when(2 * pair + e < hg)
+            def _():
+                start(q_copies(2 * pair + e) + own_copies(2 * pair + e, (1,)))
+
         return carry
 
     lax.fori_loop(0, hg, one_pair, 0)
@@ -211,65 +214,85 @@
             parts += [table[slot, pl.ds(row, 1), :]] * (tile // hd)
         return jnp.concatenate(parts, axis=1)
 
-    def attend(h, grp, size, bias, first, slots=(0, 1, 2)):
-        keys = len(bias) * size
+    def attend(h, work, slots=(0, 1, 2)):
         wide = [slice(c, c + w) for c, w in blocks if c // tile in slots]
-
-        def scores(cl):
+        lots = [(*each, wide[n : n + 2]) for each in work for n in range(0, len(wide), 2)]
+        items = [(grp, len(bias) * tile, cl) for grp, bias, first, lot in lots for cl in lot]
+
+        def scores(grp, keys, cl):
             return lax.dot_general(kbuf[h, grp, 0:keys, :], qbuf[h, cl, :], NT, preferred_element_type=F32)
 
-        def weigh(s, cl):
-            parts = [s[t * size : (t + 1) * size] for t in range(len(bias))]
+        def weigh(s, bias, first, cl, slot, span):
+            parts = [s[t * tile : (t + 1) * tile] for t in range(len(bias))]
             new = jnp.full((1, s.shape[1]), FLOOR, F32) if first else top[h, 0:1, cl]
             old = new
             for part, shift in zip(parts, bias):
                 new = jnp.maximum(new, jnp.max(part, axis=0, keepdims=True) + shift[:, cl])
-            expo = [jnp.exp2(part * scale - (new - shift[:, cl]) * scale) for part, shift in zip(parts, bias)]
-            sums = sum(jnp.sum(part, axis=0, keepdims=True) for part in expo)
+            sums = None
+            for t, (part, shift) in enumerate(zip(parts, bias)):
+                expo = jnp.exp2(part * scale - (new - shift[:, cl]) * scale)
+                pbuf[slot, t * tile : (t + 1) * tile, span] = expo.astype(BF16)
+                fold = jnp.sum(expo, axis=0, keepdims=True)
+                sums = fold if sums is None else sums + fold
             keep = None
             if not first:
                 keep = jnp.exp2((old - new) * scale)
                 sums = sums + tot[h, 0:1, cl] * keep
             tot[h, 0:1, cl] = sums
             top[h, 0:1, cl] = new
-            return keep, jnp.concatenate([part.astype(BF16) for part in expo], axis=0)
-
-        def add(keep, weight, cl):
-            new = jnp.dot(vbuf[h, grp, :, 0:keys], weight, preferred_element_type=F32)
-            acc[h, :, cl] = new if first else acc[h, :, cl] * keep + new
-
-        s = scores(wide[0])
-        for n, cl in enumerate(wide):
-            later = scores(wide[n + 1]) if n + 1 < len(wide) else None
-            keep, weight = weigh(s, cl)
-            add(keep, weight, cl)
-            s = later
+            return keep
+
+        def add(slot, grp, keys, first, lot, keeps):
+            cl = slice(lot[0].start, lot[-1].stop)
+            new = jnp.dot(
+                vbuf[h, grp, :, 0:keys], pbuf[slot, 0:keys, 0 : cl.stop - cl.start], preferred_element_type=F32
+            )
+            acc[h, :, cl] = new if first else acc[h, :, cl] * jnp.concatenate(keeps, axis=1) + new
+
+        s = scores(*items[0])
+        count = 0
+        last = None
+        for n, (grp, bias, first, lot) in enumerate(lots):
+            keeps = []
+            for cl in lot:
+                count += 1
+                later = scores(*items[count]) if count < len(items) else None
+                offset = cl.start - lot[0].start
+                keeps.append(weigh(s, bias, first, cl, n % 2, slice(offset, offset + cl.stop - cl.start)))
+                s = later
+            if last is not None:
+                add(*last)
+            last = (n % 2, grp, len(bias) * tile, first, lot, keeps)
+        add(*last)
+
+    def arrive(h, grp):
+        for e in range(2):
+            for kv in range(2):
+                dst = kv_dst(h, grp, e)[kv]
+                remote(dst, dst, own_send.at[h, 0, kv], kv_recv.at[h, grp, e, kv], partner).wait_recv()
 
     def own_step(h, carry):
         for copy in q_copies(h):
             copy.wait_recv()
-        attend(h, 0, tile, [shifts(h, 0, 0)], True)
-        return carry
-
-    lax.fori_loop(0, hg, own_step, 0)
-
-    def place(t):
-        block = t // 3
-        return 3 * ((block // 2) % 2) + t % 3, 1 + block % 2 + 2 * (block // 4)
-
-    def group_bias(h, t):
-        block = t // 3
-        late, odd = block // 4, block % 2
-        b0 = late * (1 - 2 * odd) + (1 - late) * (1 - odd)
-        b1 = late * (1 - 2 * odd) - (1 - late) * (1 - odd)
-        g0 = late + (1 - late) * odd
-        return [shifts(h, b0, g0), shifts(h, b1, 0 - g0)]
-
-    def arrive(h, grp):
-        for e in range(2):
-            for kv in range(2):
-                dst = kv_dst(h, grp, e)[kv]
-                remote(dst, dst, own_send.at[h, 0, kv], kv_recv.at[h, grp, e, kv], partner).wait_recv()
+        attend(h, [(0, [shifts(h, 0, 0)], True)])
+        return carry
+
+    def first_own(h, carry):
+        start(own_copies(h, (2,)))
+        return own_step(h, carry)
+
+    def forward(h, carry):
+        arrive(h, 1)
+        start(fwd_copies(h))
+        return carry
+
+    def send_first(h, carry):
+        start(q_copies(h) + own_copies(h, (1,)))
+        return carry
+
+    def send_second(h, carry):
+        start(own_copies(h, (2,)))
+        return carry
 
     def give_back(h):
         for e in range(2):
@@ -279,37 +302,58 @@
             ssend[h, e, 1:2, :] = tot[h, 0:1, cl]
         start(o_copies(h))
 
+    def two_groups(h, late):
+        first = [shifts(h, 1, late), shifts(h, 2 * late - 1, 0 - late)]
+        second = [shifts(h, 0 - late, 1), shifts(h, 0 - late, -1)]
+        return [(1 + 2 * late, first, False), (2 + 2 * late, second, False)]
+
     def step(t, carry):
-        h, grp = place(t)
-
-        @pl.when(t // 3 == 2)
+        block, rest = t // 3, t % 3
+        late = block % 2
+        h = 3 * (block // 2) + rest
+
+        @pl.when(t == 2)
+        def _():
+            lax.fori_loop(hg, group, send_first, 0)
+
+        @pl.when(t == 3)
+        def _():
+            lax.fori_loop(hg, group, send_second, 0)
+
+        @pl.when(t == 5)
+        def _():
+            lax.fori_loop(hg, group, forward, 0)
+
+        @pl.when(block == 2)
         def _():
             own_step(h, 0)
 
-        arrive(h, grp)
-
-        @pl.when(grp == 1)
-        def _():
-            start(fwd_copies(h))
-
-        attend(h, grp, tile, group_bias(h, t), False)
-
-        @pl.when(grp == 4)
+        @pl.when(late == 0)
+        def _():
+            arrive(h, 2)
+
+        @pl.when(late == 1)
+        def _():
+            arrive(h, 3)
+            arrive(h, 4)
+
+        attend(h, two_groups(h, late))
+
+        @pl.when(late == 1)
         def _():
             give_back(h)
 
         return carry
 
-    def last_others(t, carry):
-        h, grp = place(t)
-        arrive(h, grp)
-        attend(h, grp, tile, group_bias(h, t), False, (1, 2))
+    def last_others(h, carry):
+        arrive(h, 3)
+        arrive(h, 4)
+        attend(h, two_groups(h, 1), (1, 2))
         give_back(h)
         return carry
 
-    def last_own(t, carry):
-        h, grp = place(t)
-        attend(h, grp, tile, group_bias(h, t), False, (0,))
+    def last_own(h, carry):
+        attend(h, two_groups(h, 1), (0,))
         return carry
 
     def combine(h, carry):
@@ -348,11 +392,13 @@
         out_ref[:, span] = (outacc[:, span] + total).astype(BF16)
         return carry
 
-    lax.fori_loop(0, 21, step, 0)
-    lax.fori_loop(21, 24, last_others, 0)
+    lax.fori_loop(0, hg, first_own, 0)
+    lax.fori_loop(0, hg, forward, 0)
+    lax.fori_loop(0, 9, step, 0)
+    lax.fori_loop(hg, group, last_others, 0)
     lax.fori_loop(0, hg, combine, 0)
     att_copies[0].start()
-    lax.fori_loop(21, 24, last_own, 0)
+    lax.fori_loop(hg, group, last_own, 0)
     for copy in wo_own:
         copy.wait()
     for copy in wo_copy:
@@ -408,6 +454,7 @@
             pltpu.VMEM((7, TABLE, hd), F32),
             pltpu.VMEM((3, hg, tile, 2 * hd), F32),
             pltpu.VMEM((tile, cols), F32),
+            pltpu.VMEM((2, 2 * tile, 2 * hd), BF16),
             dma((3 + 3 * hg,)),
             dma((5,)),
             dma((5,)),

time: 86.7 us -> 80.2 us (0.925)
  Pallas kernels: 83.5 us -> 77 us
    pallas_call x1, Pallas kernels: 83.5 us -> 77 us  [on_device(): pl.pallas_call(functools.partial(kernel, blocks), out_shape=jax.ShapeDtyp...]
where the time goes in v3:
time: 80.2 us; the launch traced here: 80 us
  Pallas kernels  77 us (96%)
  local copies, waits for them, and re-layouts  2.36 us (3%)
    pallas_call x1, Pallas kernels, on_device(): pl.pallas_call(functools.partial(kernel, blocks), out_shape=jax.ShapeDtyp...  77 us
    unnamed x1, local copies, waits for them, and re-layouts  2.36 us

profile of v3, /device:TPU:1, one launch (start us, length us, event | category | flops | bytes accessed | tf_op | source)
XLA Modules:
  0.0 80.0 jit_solution(9236860158672400880)
XLA Ops:
  0.7 77.0 %tile_attention.1 = bf16[384,1536]{1,0:T(8,128)(2,1)} custom-call(bf16[384,1536]{1,0:T(8,128)(2,1)} %x_hbm.1, bf16[3072,768]{1,0:T(8,128)(2,1)} %wq_hbm.1, bf16[3072,768]{1,0:T(8,128)(2,1)} %wk_hbm.1, bf16[3072,768]{1,0:T(8,128)(2,1)} %wv_hbm.1, bf16[768,3072]{1,0:T(8,128)(2,1)} %wo_hbm.1, f32[1,128]{1,0:T(1,128)} %bitcast.4, f32[1,128]{1,0:T(1,128)} %bitcast.5, ...), custom_call_target="tpu_custom_call" | custom-call | tf_op jit(solution)/shard_map/tile_attention/pallas_call | solution.py:434
  77.7 2.4 %copy.12 = bf16[384,1536]{1,0:T(8,128)(2,1)} copy(bf16[384,1536]{1,0:T(8,128)(2,1)} %tile_attention.1) | data formatting | bytes 2359296

commit v4 on v3

--- a/solution.py
+++ b/solution.py
@@ -33,7 +33,7 @@
     blocks,
     x_hbm, wq_hbm, wk_hbm, wv_hbm, wo_hbm, qg_ref, kg_ref, ids_ref, cnt_ref,
     out_ref,
-    xbuf, wbuf, wobuf, kbuf, vbuf, qbuf, acc, top, tot, osend, orecv, ssend, srecv, attbuf, table, partial, outacc, pbuf,
+    xbuf, wbuf, wobuf, kbuf, vbuf, qbuf, acc, top, tot, osend, orecv, ssend, srecv, attbuf, table, partial, outacc,
     load_sem, pair_send, pair_recv, tab_send, tab_recv,
     own_send, fwd_send, kv_recv, q_send, q_recv, o_send, o_recv,
 ):
@@ -169,8 +169,6 @@
             partial[kind, pair] = jnp.dot(xbuf[half], wbuf[kind, pair, rows], preferred_element_type=F32)
         return carry
 
-    lax.fori_loop(0, hg, own_half, 0)
-    x_copy.wait_recv()
 
     def project(kind, pair):
         rows = pl.ds(pl.multiple_of((1 - half) * cols, cols), cols)
@@ -190,15 +188,22 @@
         proj = project(1, pair)
         for e in range(2):
             vbuf[2 * pair + e, 0, :, 0:tile] = jnp.transpose(proj[:, e * hd : (e + 1) * hd]).astype(BF16)
-        for e in range(2):
-
-            @pl.when(2 * pair + e < hg)
-            def _():
-                start(q_copies(2 * pair + e) + own_copies(2 * pair + e, (1,)))
-
-        return carry
-
-    lax.fori_loop(0, hg, one_pair, 0)
+        @pl.when(pair == 0)
+        def _():
+            for h in range(2):
+                start(q_copies(h) + own_copies(h, (1,)))
+
+        @pl.when(pair == 1)
+        def _():
+            start(q_copies(2) + own_copies(2, (1,)))
+
+        return carry
+
+    lax.fori_loop(0, hg - 1, own_half, 0)
+    x_copy.wait_recv()
+    lax.fori_loop(0, hg - 1, one_pair, 0)
+    own_half(hg - 1, 0)
+    one_pair(hg - 1, 0)
     start(wo_own)
     start(wo_copy)
     for copy in tab_copies:
@@ -219,50 +224,56 @@
         lots = [(*each, wide[n : n + 2]) for each in work for n in range(0, len(wide), 2)]
         items = [(grp, len(bias) * tile, cl) for grp, bias, first, lot in lots for cl in lot]
 
-        def scores(grp, keys, cl):
-            return lax.dot_general(kbuf[h, grp, 0:keys, :], qbuf[h, cl, :], NT, preferred_element_type=F32)
-
-        def weigh(s, bias, first, cl, slot, span):
-            parts = [s[t * tile : (t + 1) * tile] for t in range(len(bias))]
-            new = jnp.full((1, s.shape[1]), FLOOR, F32) if first else top[h, 0:1, cl]
+        def scores(grp, keys, cl, t):
+            rows = slice(t * tile, (t + 1) * tile)
+            return lax.dot_general(kbuf[h, grp, rows, :], qbuf[h, cl, :], NT, preferred_element_type=F32)
+
+        def weigh(parts, bias, first, cl, following):
+            later = []
+            ahead = following[1] // tile if following else 0
+            new = jnp.full((1, parts[0].shape[1]), FLOOR, F32) if first else top[h, 0:1, cl]
             old = new
             for part, shift in zip(parts, bias):
                 new = jnp.maximum(new, jnp.max(part, axis=0, keepdims=True) + shift[:, cl])
             sums = None
-            for t, (part, shift) in enumerate(zip(parts, bias)):
+            weights = []
+            for part, shift in zip(parts, bias):
+                if len(later) < ahead:
+                    later.append(scores(*following, len(later)))
                 expo = jnp.exp2(part * scale - (new - shift[:, cl]) * scale)
-                pbuf[slot, t * tile : (t + 1) * tile, span] = expo.astype(BF16)
+                weights.append(expo.astype(BF16))
                 fold = jnp.sum(expo, axis=0, keepdims=True)
                 sums = fold if sums is None else sums + fold
+            while len(later) < ahead:
+                later.append(scores(*following, len(later)))
             keep = None
             if not first:
                 keep = jnp.exp2((old - new) * scale)
                 sums = sums + tot[h, 0:1, cl] * keep
             tot[h, 0:1, cl] = sums
             top[h, 0:1, cl] = new
-            return keep
-
-        def add(slot, grp, keys, first, lot, keeps):
+            return keep, jnp.concatenate(weights, axis=0), later
+
+        def add(grp, keys, first, lot, done):
             cl = slice(lot[0].start, lot[-1].stop)
             new = jnp.dot(
-                vbuf[h, grp, :, 0:keys], pbuf[slot, 0:keys, 0 : cl.stop - cl.start], preferred_element_type=F32
+                vbuf[h, grp, :, 0:keys], jnp.concatenate([each[1] for each in done], axis=1), preferred_element_type=F32
             )
-            acc[h, :, cl] = new if first else acc[h, :, cl] * jnp.concatenate(keeps, axis=1) + new
-
-        s = scores(*items[0])
+            acc[h, :, cl] = new if first else acc[h, :, cl] * jnp.concatenate([each[0] for each in done], axis=1) + new
+
+        s = [scores(*items[0], t) for t in range(items[0][1] // tile)]
         count = 0
         last = None
-        for n, (grp, bias, first, lot) in enumerate(lots):
-            keeps = []
+        for grp, bias, first, lot in lots:
+            done = []
             for cl in lot:
                 count += 1
-                later = scores(*items[count]) if count < len(items) else None
-                offset = cl.start - lot[0].start
-                keeps.append(weigh(s, bias, first, cl, n % 2, slice(offset, offset + cl.stop - cl.start)))
-                s = later
+                following = items[count] if count < len(items) else None
+                done.append(weigh(s, bias, first, cl, following))
+                s = done[-1][2]
             if last is not None:
                 add(*last)
-            last = (n % 2, grp, len(bias) * tile, first, lot, keeps)
+            last = (grp, len(bias) * tile, first, lot, done)
         add(*last)
 
     def arrive(h, grp):
@@ -271,23 +282,26 @@
                 dst = kv_dst(h, grp, e)[kv]
                 remote(dst, dst, own_send.at[h, 0, kv], kv_recv.at[h, grp, e, kv], partner).wait_recv()
 
-    def own_step(h, carry):
+    def own_alone(h, carry):
+        attend(h, [(0, [shifts(h, 0, 0)], True)], (0,))
+        return carry
+
+    def own_others(h, carry):
         for copy in q_copies(h):
             copy.wait_recv()
-        attend(h, [(0, [shifts(h, 0, 0)], True)])
-        return carry
-
-    def first_own(h, carry):
-        start(own_copies(h, (2,)))
-        return own_step(h, carry)
+        attend(h, [(0, [shifts(h, 0, 0)], True)], (1, 2))
+        return carry
 
     def forward(h, carry):
-        arrive(h, 1)
         start(fwd_copies(h))
         return carry
 
+    def send_queries(h, carry):
+        start(q_copies(h))
+        return carry
+
     def send_first(h, carry):
-        start(q_copies(h) + own_copies(h, (1,)))
+        start(own_copies(h, (1,)))
         return carry
 
     def send_second(h, carry):
@@ -307,35 +321,34 @@
         second = [shifts(h, 0 - late, 1), shifts(h, 0 - late, -1)]
         return [(1 + 2 * late, first, False), (2 + 2 * late, second, False)]
 
+    def one_group(t, carry):
+        block, h = t // 3, t % 3
+        arrive(h, 1 + block)
+
+        @pl.when(t == 1)
+        def _():
+            lax.fori_loop(hg, group, send_queries, 0)
+
+        @pl.when(t == 2)
+        def _():
+            lax.fori_loop(hg, group, send_first, 0)
+
+        @pl.when(t == 4)
+        def _():
+            lax.fori_loop(hg, group, send_second, 0)
+
+        attend(h, [(1 + block, [shifts(h, 1 - block, block), shifts(h, block - 1, 0 - block)], False)])
+        return carry
+
     def step(t, carry):
-        block, rest = t // 3, t % 3
-        late = block % 2
-        h = 3 * (block // 2) + rest
+        late, rest = t // 3, t % 3
+        h = 3 * (1 - late) + rest
+        arrive(h, 1 + 2 * late)
+        arrive(h, 2 + 2 * late)
 
         @pl.when(t == 2)
         def _():
-            lax.fori_loop(hg, group, send_first, 0)
-
-        @pl.when(t == 3)
-        def _():
-            lax.fori_loop(hg, group, send_second, 0)
-
-        @pl.when(t == 5)
-        def _():
             lax.fori_loop(hg, group, forward, 0)
-
-        @pl.when(block == 2)
-        def _():
-            own_step(h, 0)
-
-        @pl.when(late == 0)
-        def _():
-            arrive(h, 2)
-
-        @pl.when(late == 1)
-        def _():
-            arrive(h, 3)
-            arrive(h, 4)
 
         attend(h, two_groups(h, late))
 
@@ -377,24 +390,35 @@
         for wave in range(2)
     ]
 
-    def project_out(wave, c):
-        span = pl.ds(pl.multiple_of(c * width, width), width)
-        total = jnp.dot(attbuf[wave, 0], wobuf[wave, 0:part, span], preferred_element_type=F32)
-        return span, total + jnp.dot(attbuf[wave, 1], wobuf[wave, part:, span], preferred_element_type=F32)
+    def project_out(wave, side, span):
+        rows = pl.ds(pl.multiple_of(side * part, part), part)
+        return jnp.dot(attbuf[wave, side], wobuf[wave, rows, span], preferred_element_type=F32)
+
+    def column(c):
+        return pl.ds(pl.multiple_of(c * width, width), width)
 
     def out_first(c, carry):
-        span, total = project_out(0, c)
-        outacc[:, span] = total
+        span = column(c)
+        outacc[:, span] = project_out(0, 0, span) + project_out(0, 1, span)
         return carry
 
     def out_second(c, carry):
-        span, total = project_out(1, c)
-        out_ref[:, span] = (outacc[:, span] + total).astype(BF16)
-        return carry
-
-    lax.fori_loop(0, hg, first_own, 0)
+        span = column(c)
+        outacc[:, span] = outacc[:, span] + project_out(1, half, span)
+        return carry
+
+    def out_third(c, carry):
+        span = column(c)
+        out_ref[:, span] = (outacc[:, span] + project_out(1, 1 - half, span)).astype(BF16)
+        return carry
+
+    lax.fori_loop(0, group, own_alone, 0)
+    lax.fori_loop(0, hg, send_second, 0)
+    lax.fori_loop(0, hg, own_others, 0)
+    lax.fori_loop(0, 6, one_group, 0)
     lax.fori_loop(0, hg, forward, 0)
-    lax.fori_loop(0, 9, step, 0)
+    lax.fori_loop(hg, group, own_others, 0)
+    lax.fori_loop(0, 6, step, 0)
     lax.fori_loop(hg, group, last_others, 0)
     lax.fori_loop(0, hg, combine, 0)
     att_copies[0].start()
@@ -407,8 +431,9 @@
     lax.fori_loop(0, cols // width, out_first, 0)
     lax.fori_loop(hg, group, combine, 0)
     att_copies[1].start()
+    lax.fori_loop(0, cols // width, out_second, 0)
     att_copies[1].wait_recv()
-    lax.fori_loop(0, cols // width, out_second, 0)
+    lax.fori_loop(0, cols // width, out_third, 0)
 
     x_copy.wait_send()
     for copy in wo_copy + att_copies + tab_copies:
@@ -454,7 +479,6 @@
             pltpu.VMEM((7, TABLE, hd), F32),
             pltpu.VMEM((3, hg, tile, 2 * hd), F32),
             pltpu.VMEM((tile, cols), F32),
-            pltpu.VMEM((2, 2 * tile, 2 * hd), BF16),
             dma((3 + 3 * hg,)),
             dma((5,)),
             dma((5,)),

time: 80.2 us -> 77 us (0.960)
  Pallas kernels: 77 us -> 73.8 us
    pallas_call x1, Pallas kernels: 77 us -> 73.8 us  [on_device(): pl.pallas_call(functools.partial(kernel, blocks), out_shape=jax.ShapeDtyp...]
where the time goes in v4:
time: 77 us; the launch traced here: 76.8 us
  Pallas kernels  73.8 us (96%)
  local copies, waits for them, and re-layouts  2.36 us (3%)
    pallas_call x1, Pallas kernels, on_device(): pl.pallas_call(functools.partial(kernel, blocks), out_shape=jax.ShapeDtyp...  73.8 us
    unnamed x1, local copies, waits for them, and re-layouts  2.36 us

profile of v4, /device:TPU:1, one launch (start us, length us, event | category | flops | bytes accessed | tf_op | source)
XLA Modules:
  0.0 76.8 jit_solution(15646640848644106813)
XLA Ops:
  0.7 73.8 %tile_attention.1 = bf16[384,1536]{1,0:T(8,128)(2,1)} custom-call(bf16[384,1536]{1,0:T(8,128)(2,1)} %x_hbm.1, bf16[3072,768]{1,0:T(8,128)(2,1)} %wq_hbm.1, bf16[3072,768]{1,0:T(8,128)(2,1)} %wk_hbm.1, bf16[3072,768]{1,0:T(8,128)(2,1)} %wv_hbm.1, bf16[768,3072]{1,0:T(8,128)(2,1)} %wo_hbm.1, f32[1,128]{1,0:T(1,128)} %bitcast.4, f32[1,128]{1,0:T(1,128)} %bitcast.5, ...), custom_call_target="tpu_custom_call" | custom-call | tf_op jit(solution)/shard_map/tile_attention/pallas_call | solution.py:459
  74.4 2.4 %copy.12 = bf16[384,1536]{1,0:T(8,128)(2,1)} copy(bf16[384,1536]{1,0:T(8,128)(2,1)} %tile_attention.1) | data formatting | bytes 2359296
